TPU v7x, 512 devices: a whole 4x8x8 slice. The times are simulated.
512 devices in a mesh: gx: 32 (over y_hi, z, core), gy: 16 (over y_lo, x).
Axes of the slice: x: 4, y: 8 (y_hi: 2, y_lo: 4; y = y_hi * 4 + y_lo), z: 8, core: 2. Of those that a mesh axis runs over, the one named last changes fastest.
Arguments:
- pressure0: float32 [4, 512, 2048], P(None, 'gx', 'gy'), may hold values from -6 to 6
- saturation0: float32 [4, 512, 2048], P(None, 'gx', 'gy'), may hold values from 0.1 to 0.9
- trans_x: float32 [4, 512, 2048], P(None, 'gx', 'gy'), may hold values from 0.1 to 2
- trans_y: float32 [4, 512, 2048], P(None, 'gx', 'gy'), may hold values from 0.1 to 2
- trans_z: float32 [3, 512, 2048], P(None, 'gx', 'gy'), may hold values from 0.05 to 1
- pore_volume: float32 [4, 512, 2048], P(None, 'gx', 'gy'), may hold values from 0.5 to 2
- upwind: int32 [4, 512, 2048], P(None, 'gx', 'gy'), may hold values from 0 to 63
- well_cell: int32 [32, 16, 64], P('gx', 'gy'), may hold values from 0 to 8191
- well_rate: float32 [32, 16, 64], P('gx', 'gy'), may hold values from -8 to 8
- plan: int32 [2, 32, 16, 64], P(None, 'gx', 'gy'), may hold values from 0 to 2
- observed: float32 [2, 2, 32, 16, 64], P(None, None, 'gx', 'gy'), may hold values from -6 to 6
Outputs:
- grad_x: float32 [4, 512, 2048], P(None, 'gx', 'gy')
- grad_y: float32 [4, 512, 2048], P(None, 'gx', 'gy')
- grad_z: float32 [3, 512, 2048], P(None, 'gx', 'gy')
Inputs may be any that keep to these rules, and one draw needn't show every extreme that they name: `upwind`: bit 3 n + d of an entry is 1 where the cell itself is upstream of its forward face along x, y or layers (d = 0, 1, 2) in step n, 0 where the next cell is. `well_cell`: a cell of the well's own tile, numbered layer by layer, then row, then column. `plan`: 0 shut, 1 half rate, 2 full rate.
All inputs are finite; a program needn't handle non-finite values.
Results may differ from a plain program's by a relative error of at most 0.0001.
Values sent between devices are 32-bit elements; how exact they have to be, the bound alone decides.
A program may use at most 64 MiB of HBM per device.

v0:
```python
import jax
import jax.numpy as jnp
from jax import lax
from jax.sharding import PartitionSpec as P

storage_coef = 1.0
time_step = 0.05


def extended(cells, sides, width):
    for axis, dim in sides:
        count = lax.axis_size(axis)
        ends = count - 1
        head = lax.slice_in_dim(cells, 0, width, axis=dim)
        tail = lax.slice_in_dim(cells, cells.shape[dim] - width, cells.shape[dim], axis=dim)
        cells = jnp.concatenate(
            [
                lax.ppermute(tail, axis, [(i, (i + 1) % count) for i in range(ends)]),
                cells,
                lax.ppermute(head, axis, [((i + 1) % count, i) for i in range(ends)]),
            ],
            axis=dim,
        )
    return cells


def shifted(value, axis, by):
    peers = lax.axis_size(axis)
    pairs = [(i, i + by) for i in range(peers) if 0 <= i + by < peers]
    return lax.ppermute(value, axis, pairs)


def mobility(saturation):
    wetted = saturation * saturation
    return wetted / (wetted + 0.5 * (1.0 - saturation) * (1.0 - saturation))


def vertical(center, faces):
    empty_layer = jnp.zeros_like(center[:1])
    upper_cells = jnp.concatenate([center[1:], empty_layer], axis=0)
    lower_cells = jnp.concatenate([empty_layer, center[:-1]], axis=0)
    face_up = jnp.concatenate([faces, empty_layer], axis=0)
    face_down = jnp.concatenate([empty_layer, faces], axis=0)
    return (face_up, face_down, upper_cells, lower_cells)


def jacobi(pressure, pressure_old, trans_x, trans_y, trans_z, pore_space, source, outside):
    center = pressure[:, 1:-1, 1:-1]
    east_face = trans_x[:, 1:-1, 1:-1]
    west_face = trans_x[:, :-2, 1:-1]
    north_face = trans_y[:, 1:-1, 1:-1]
    south_face = trans_y[:, 1:-1, :-2]
    face_up, face_down, upper_cells, lower_cells = vertical(center, trans_z[:, 1:-1, 1:-1])
    storage = storage_coef * pore_space[:, 1:-1, 1:-1]
    numerator = (
        storage * pressure_old[:, 1:-1, 1:-1]
        + source[:, 1:-1, 1:-1]
        + east_face * pressure[:, 2:, 1:-1]
        + west_face * pressure[:, :-2, 1:-1]
        + north_face * pressure[:, 1:-1, 2:]
        + south_face * pressure[:, 1:-1, :-2]
        + face_up * upper_cells
        + face_down * lower_cells
    )
    denominator = (
        storage
        + east_face
        + west_face
        + north_face
        + south_face
        + face_up
        + face_down
        + outside[:, 1:-1, 1:-1]
    )
    return numerator / denominator


def transport(
    pressure,
    saturation,
    trans_x,
    trans_y,
    trans_z,
    upwind_x,
    upwind_y,
    upwind_z,
    pore_space,
    outside,
):
    mobile = mobility(saturation)
    flux_x = (pressure[:, :-1, :] - pressure[:, 1:, :]) * (
        upwind_x[:, :-1, :] * mobile[:, :-1, :]
        + (trans_x[:, :-1, :] - upwind_x[:, :-1, :]) * mobile[:, 1:, :]
    )
    flux_y = (pressure[:, :, :-1] - pressure[:, :, 1:]) * (
        upwind_y[:, :, :-1] * mobile[:, :, :-1]
        + (trans_y[:, :, :-1] - upwind_y[:, :, :-1]) * mobile[:, :, 1:]
    )
    mid_pressure = pressure[:, 1:-1, 1:-1]
    mid_mobile = mobile[:, 1:-1, 1:-1]
    rise_upwind = upwind_z[:, 1:-1, 1:-1]
    rise_trans = trans_z[:, 1:-1, 1:-1]
    flux_z = (mid_pressure[:-1] - mid_pressure[1:]) * (
        rise_upwind * mid_mobile[:-1] + (rise_trans - rise_upwind) * mid_mobile[1:]
    )
    empty_layer = jnp.zeros_like(mid_pressure[:1])
    net_outflow = (
        flux_x[:, 1:, 1:-1]
        - flux_x[:, :-1, 1:-1]
        + flux_y[:, 1:-1, 1:]
        - flux_y[:, 1:-1, :-1]
        + jnp.concatenate([flux_z, empty_layer], axis=0)
        - jnp.concatenate([empty_layer, flux_z], axis=0)
    )
    return saturation[:, 1:-1, 1:-1] - time_step * net_outflow / (
        pore_space[:, 1:-1, 1:-1] + outside[:, 1:-1, 1:-1]
    )


def pieces(coef, layers, step_index, steps):

    def block_of(number):
        return coef[number * layers : (number + 1) * layers]

    first_up = 4 + steps + 3 * step_index
    return (
        block_of(0),
        block_of(1),
        block_of(2)[: layers - 1],
        block_of(3),
        block_of(4 + step_index),
        block_of(first_up),
        block_of(first_up + 1),
        block_of(first_up + 2)[: layers - 1],
    )


def relax(pressure, pressure_old, coef, outside, layers, step_index, steps):
    parts = pieces(coef, layers, step_index, steps)
    return jacobi(pressure, pressure_old, parts[0], parts[1], parts[2], parts[3], parts[4], outside)


def advect(pair, coef, outside, layers, step_index, steps):
    parts = pieces(coef, layers, step_index, steps)
    return transport(
        pair[:layers],
        pair[layers:],
        parts[0],
        parts[1],
        parts[2],
        parts[5],
        parts[6],
        parts[7],
        parts[3],
        outside,
    )


def extend(stack, width):
    return extended(stack, (("gx", 1), ("gy", 2)), width)


def fold_back(cotangent, width):
    row_count = cotangent.shape[1]
    from_upper = shifted(cotangent[:, :width, :], "gx", -1)
    from_lower = shifted(cotangent[:, row_count - width :, :], "gx", 1)
    cotangent = cotangent.at[:, row_count - 2 * width : row_count - width, :].add(from_upper)
    cotangent = cotangent.at[:, width : 2 * width, :].add(from_lower)
    cotangent = cotangent[:, width : row_count - width, :]
    col_count = cotangent.shape[2]
    from_right = shifted(cotangent[:, :, :width], "gy", -1)
    from_left = shifted(cotangent[:, :, col_count - width :], "gy", 1)
    cotangent = cotangent.at[:, :, col_count - 2 * width : col_count - width].add(from_right)
    cotangent = cotangent.at[:, :, width : 2 * width].add(from_left)
    return cotangent[:, :, width : col_count - width]


def on_device(
    pressure0,
    saturation0,
    trans_x,
    trans_y,
    trans_z,
    pore_volume,
    upwind,
    well_cell,
    well_rate,
    plan,
    observed,
):
    layers, row_count, col_count = pressure0.shape
    steps = plan.shape[0]
    depth = 1
    total_rows = row_count * lax.axis_size("gx")
    total_cols = col_count * lax.axis_size("gy")
    row_ids = lax.axis_index("gx") * row_count + lax.broadcasted_iota(jnp.int32, pressure0.shape, 1)
    col_ids = lax.axis_index("gy") * col_count + lax.broadcasted_iota(jnp.int32, pressure0.shape, 2)
    keep_x = row_ids < total_rows - 1
    keep_y = col_ids < total_cols - 1
    trans_xe = jnp.where(keep_x, trans_x, 0.0)
    trans_ye = jnp.where(keep_y, trans_y, 0.0)
    trans_zf = jnp.concatenate([trans_z, jnp.zeros((1, row_count, col_count), jnp.float32)], axis=0)
    cells = well_cell.reshape(-1)
    flat_size = layers * row_count * col_count
    sources = []
    upwinds = []
    bits_all = []
    for step_index in range(steps):
        rates = well_rate.reshape(-1) * plan[step_index].reshape(-1).astype(jnp.float32) * 0.5
        sources.append(
            jnp.zeros((flat_size,), jnp.float32).at[cells].add(rates).reshape(pressure0.shape)
        )
        bits = [
            jnp.bitwise_and(jnp.right_shift(upwind, 3 * step_index + direction), 1).astype(
                jnp.float32
            )
            for direction in range(3)
        ]
        bits_all.append(bits)
        upwinds += [trans_xe * bits[0], trans_ye * bits[1], trans_zf * bits[2]]
    coef = extend(
        jnp.concatenate([trans_xe, trans_ye, trans_zf, pore_volume] + sources + upwinds, axis=0),
        depth,
    )
    padded_shape = (1, row_count + 2 * depth, col_count + 2 * depth)
    grow_rows = (
        lax.axis_index("gx") * row_count - depth + lax.broadcasted_iota(jnp.int32, padded_shape, 1)
    )
    grow_cols = (
        lax.axis_index("gy") * col_count - depth + lax.broadcasted_iota(jnp.int32, padded_shape, 2)
    )
    beyond = (
        (grow_rows < 0) | (grow_rows >= total_rows) | (grow_cols < 0) | (grow_cols >= total_cols)
    )
    outside = jnp.where(beyond, 1.0, 0.0).astype(jnp.float32)
    state = jnp.concatenate([pressure0, saturation0], axis=0)
    saved = []
    well_grads = []
    for step_index in range(steps):
        padded = extend(state[:layers], depth)
        first = relax(padded, padded, coef, outside, layers, step_index, steps)
        padded_first = extend(first, depth)
        second = relax(padded_first, padded, coef, outside, layers, step_index, steps)
        pair = extend(jnp.concatenate([second, state[layers:]], axis=0), depth)
        state = jnp.concatenate(
            [second, advect(pair, coef, outside, layers, step_index, steps)], axis=0
        )
        saved.append((padded, padded_first, pair))
        flat_state = state.reshape(2, -1)
        miss_p = flat_state[0][cells] - observed[step_index, 0].reshape(-1)
        miss_s = flat_state[1][cells] - observed[step_index, 1].reshape(-1)
        zero_flat = jnp.zeros((flat_size,), jnp.float32)
        well_grads.append(
            jnp.concatenate(
                [zero_flat.at[cells].add(miss_p), zero_flat.at[cells].add(miss_s)]
            ).reshape(state.shape)
        )
    carried = jnp.zeros_like(state)
    coef_grad = jnp.zeros_like(coef)
    for step_index in reversed(range(steps)):
        carried = carried + well_grads[step_index]
        padded, padded_first, pair = saved[step_index]
        _, back_move = jax.vjp(
            lambda pair_in, coef_in: advect(pair_in, coef_in, outside, layers, step_index, steps),
            pair,
            coef,
        )
        pair_grad, step_coef = back_move(carried[layers:])
        coef_grad = coef_grad + step_coef
        returned = fold_back(pair_grad, depth)
        press_grad = carried[:layers] + returned[:layers]
        sat_grad = returned[layers:]
        _, back_second = jax.vjp(
            lambda first_in, old_in, coef_in: relax(
                first_in, old_in, coef_in, outside, layers, step_index, steps
            ),
            padded_first,
            padded,
            coef,
        )
        first_grad, old_grad, step_coef = back_second(press_grad)
        coef_grad = coef_grad + step_coef
        first_grad = fold_back(first_grad, depth)
        _, back_first = jax.vjp(
            lambda start_in, coef_in: relax(
                start_in, start_in, coef_in, outside, layers, step_index, steps
            ),
            padded,
            coef,
        )
        start_grad, step_coef = back_first(first_grad)
        coef_grad = coef_grad + step_coef
        carried = jnp.concatenate([fold_back(start_grad + old_grad, depth), sat_grad], axis=0)
    wanted = [0, 1, 2] + list(range(4 + steps, 4 + 4 * steps))
    returned = fold_back(
        jnp.concatenate(
            [coef_grad[number * layers : (number + 1) * layers] for number in wanted], axis=0
        ),
        depth,
    )

    def field_of(number):
        return returned[number * layers : (number + 1) * layers]

    grad_x = field_of(0)
    grad_y = field_of(1)
    grad_z = field_of(2)
    for step_index in range(steps):
        bits = bits_all[step_index]
        grad_x = grad_x + bits[0] * field_of(3 + 3 * step_index)
        grad_y = grad_y + bits[1] * field_of(4 + 3 * step_index)
        grad_z = grad_z + bits[2] * field_of(5 + 3 * step_index)
    grad_x = jnp.where(keep_x, grad_x, 0.0)
    grad_y = jnp.where(keep_y, grad_y, 0.0)
    return (grad_x, grad_y, grad_z[: layers - 1])


def solution(mesh):
    in_specs = (
        P(None, "gx", "gy"),
        P(None, "gx", "gy"),
        P(None, "gx", "gy"),
        P(None, "gx", "gy"),
        P(None, "gx", "gy"),
        P(None, "gx", "gy"),
        P(None, "gx", "gy"),
        P("gx", "gy", None),
        P("gx", "gy", None),
        P(None, "gx", "gy", None),
        P(None, None, "gx", "gy", None),
    )
    out_specs = (P(None, "gx", "gy"), P(None, "gx", "gy"), P(None, "gx", "gy"))
    return jax.shard_map(
        on_device, mesh=mesh, in_specs=in_specs, out_specs=out_specs, check_vma=False
    )
```

profile of v0, /device:TPU:56, one launch (start us, length us, event | category | flops | bytes accessed | tf_op | source)
XLA Modules:
  0.0 359.0 jit_solution(9022286767617607907)
XLA Ops:
  13.9 12.6 %collective-permute-start.4 = (f32[48,1,128]{2,1,0:T(1,128)S(1)}, f32[48,1,128]{2,1,0:T(1,128)S(1)}, u32[]{:S(2)}, u32[]{:S(2)}) collective-permute-start(f32[48,1,128]{2,1,0:T(1,128)S(1)} %get-tuple-element.392), channel_id=1, source_target_pairs={{16,0},{32,16},{48,32},{64,48},{80,64},{96,80},{112,96},{128,112},... | collective-permute-start | bytes 73736 | tf_op jit(solution)/shard_map/ppermute | solution.py:20
  26.5 2.6 collective-permute-start
  31.3 8.8 %collective-permute-done.2 = f32[4,1,128]{2,1,0:T(1,128)S(1)} collective-permute-done((f32[4,1,128]{2,1,0:T(1,128)S(1)}, f32[4,1,128]{2,1,0:T(1,128)S(1)}, u32[]{:S(2)}, u32[]{:S(2)}) %collective-permute-start.2) | collective-permute-done | bytes 2080 | tf_op jit(solution)/shard_map/ppermute | solution.py:18
  40.2 4.4 %collective-permute-start.3 = (f32[4,18,1]{2,1,0:T(8,128)S(1)}, f32[4,18,1]{2,1,0:T(8,128)S(1)}, u32[]{:S(2)}, u32[]{:S(2)}) collective-permute-start(f32[4,18,1]{2,1,0:T(8,128)S(1)} %get-tuple-element.482), channel_id=1, source_target_pairs={{1,0},{2,1},{3,2},{4,3},{5,4},{6,5},{7,6},{8,7},{9,8},{10,9},{11,1... | collective-permute-start | bytes 872 | tf_op jit(solution)/shard_map/ppermute | solution.py:20
  47.3 2.8 collective-permute-start.5
  50.1 4.8 %collective-permute-done.5 = f32[48,18,1]{0,1,2:T(8,128)S(1)} collective-permute-done((f32[48,18,1]{0,1,2:T(8,128)S(1)}, f32[48,18,1]{0,1,2:T(8,128)S(1)}, u32[]{:S(2)}, u32[]{:S(2)}) %collective-permute-start.5) | collective-permute-done | bytes 3488 | tf_op jit(solution)/shard_map/ppermute | solution.py:18
  56.1 2.0 collective-permute-start.7
  58.2 2.4 collective-permute-start.8
  60.8 3.9 %collective-permute-start.23 = (f32[48,18,1]{0,1,2:T(8,128)S(1)}, f32[48,18,1]{0,1,2:T(8,128)S(1)}, u32[]{:S(2)}, u32[]{:S(2)}) collective-permute-start(f32[48,18,1]{0,1,2:T(8,128)S(1)} %copy.64), channel_id=1, source_target_pairs={{1,0},{2,1},{3,2},{4,3},{5,4},{6,5},{7,6},{8,7},{9,8},{10,9},{11,1... | collective-permute-start | bytes 10376 | tf_op jit(solution)/shard_map/ppermute | solution.py:20
  64.8 4.3 %collective-permute-done.8 = f32[4,1,128]{2,1,0:T(1,128)S(1)} collective-permute-done((f32[4,1,128]{2,1,0:T(1,128)S(1)}, f32[4,1,128]{2,1,0:T(1,128)S(1)}, u32[]{:S(2)}, u32[]{:S(2)}) %collective-permute-start.8) | collective-permute-done | bytes 2080 | tf_op jit(solution)/shard_map/ppermute | solution.py:18
  71.1 6.0 %collective-permute-start.9 = (f32[4,18,1]{2,1,0:T(8,128)S(1)}, f32[4,18,1]{2,1,0:T(8,128)S(1)}, u32[]{:S(2)}, u32[]{:S(2)}) collective-permute-start(f32[4,18,1]{2,1,0:T(8,128)S(1)} %get-tuple-element.480), channel_id=1, source_target_pairs={{1,0},{2,1},{3,2},{4,3},{5,4},{6,5},{7,6},{8,7},{9,8},{10,9},{11,1... | collective-permute-start | bytes 872 | tf_op jit(solution)/shard_map/ppermute | solution.py:20
  79.6 3.5 collective-permute-start.11
  87.0 9.7 %collective-permute-start.20 = (f32[8,1,128]{2,1,0:T(1,128)S(1)}, f32[8,1,128]{2,1,0:T(1,128)S(1)}, u32[]{:S(2)}, u32[]{:S(2)}) collective-permute-start(f32[8,1,128]{2,1,0:T(1,128)S(1)} %get-tuple-element.465), channel_id=1, source_target_pairs={{16,0},{32,16},{48,32},{64,48},{80,64},{96,80},{112,96},{128,112},... | collective-permute-start | bytes 12296 | tf_op jit(solution)/shard_map/ppermute | solution.py:20
  100.0 6.1 %collective-permute-start.22 = (f32[8,18,1]{2,1,0:T(8,128)S(1)}, f32[8,18,1]{2,1,0:T(8,128)S(1)}, u32[]{:S(2)}, u32[]{:S(2)}) collective-permute-start(f32[8,18,1]{2,1,0:T(8,128)S(1)} %get-tuple-element.445), channel_id=1, source_target_pairs={{1,0},{2,1},{3,2},{4,3},{5,4},{6,5},{7,6},{8,7},{9,8},{10,9},{11,1... | collective-permute-start | bytes 1736 | tf_op jit(solution)/shard_map/ppermute | solution.py:20
  106.2 3.9 %collective-permute-start.13 = (f32[4,18,1]{2,1,0:T(8,128)S(1)}, f32[4,18,1]{2,1,0:T(8,128)S(1)}, u32[]{:S(2)}, u32[]{:S(2)}) collective-permute-start(f32[4,18,1]{2,1,0:T(8,128)S(1)} %get-tuple-element.478), channel_id=1, source_target_pairs={{1,0},{2,1},{3,2},{4,3},{5,4},{6,5},{7,6},{8,7},{9,8},{10,9},{11,1... | collective-permute-start | bytes 872 | tf_op jit(solution)/shard_map/ppermute | solution.py:20
  113.0 5.2 %collective-permute-done.14 = f32[4,18,1]{2,1,0:T(8,128)S(1)} collective-permute-done((f32[4,18,1]{2,1,0:T(8,128)S(1)}, f32[4,18,1]{2,1,0:T(8,128)S(1)}, u32[]{:S(2)}, u32[]{:S(2)}) %collective-permute-start.14) | collective-permute-done | bytes 320 | tf_op jit(solution)/shard_map/ppermute | solution.py:18
  118.9 7.6 %collective-permute-start.15 = (f32[4,1,128]{2,1,0:T(1,128)S(1)}, f32[4,1,128]{2,1,0:T(1,128)S(1)}, u32[]{:S(2)}, u32[]{:S(2)}) collective-permute-start(f32[4,1,128]{2,1,0:T(1,128)S(1)} %get-tuple-element.510), channel_id=1, source_target_pairs={{16,0},{32,16},{48,32},{64,48},{80,64},{96,80},{112,96},{128,112},... | collective-permute-start | bytes 6152 | tf_op jit(solution)/shard_map/ppermute | solution.py:20
  130.4 7.1 %collective-permute-done.16 = f32[4,1,128]{2,1,0:T(1,128)S(1)} collective-permute-done((f32[4,1,128]{2,1,0:T(1,128)S(1)}, f32[4,1,128]{2,1,0:T(1,128)S(1)}, u32[]{:S(2)}, u32[]{:S(2)}) %collective-permute-start.16) | collective-permute-done | bytes 2080 | tf_op jit(solution)/shard_map/ppermute | solution.py:18
  139.5 3.9 %collective-permute-start.18 = (f32[4,18,1]{2,1,0:T(8,128)S(1)}, f32[4,18,1]{2,1,0:T(8,128)S(1)}, u32[]{:S(2)}, u32[]{:S(2)}) collective-permute-start(f32[4,18,1]{2,1,0:T(8,128)S(1)} %get-tuple-element.477), channel_id=1, source_target_pairs={{0,1},{1,2},{2,3},{3,4},{4,5},{5,6},{6,7},{7,8},{8,9},{9,10},{10,1... | collective-permute-start | bytes 872 | tf_op jit(solution)/shard_map/ppermute | solution.py:18
  143.6 4.0 %collective-permute-done.18 = f32[4,18,1]{2,1,0:T(8,128)S(1)} collective-permute-done((f32[4,18,1]{2,1,0:T(8,128)S(1)}, f32[4,18,1]{2,1,0:T(8,128)S(1)}, u32[]{:S(2)}, u32[]{:S(2)}) %collective-permute-start.18) | collective-permute-done | bytes 320 | tf_op jit(solution)/shard_map/ppermute | solution.py:18
  150.3 9.7 %collective-permute-start.25 = (f32[8,1,128]{2,1,0:T(1,128)S(1)}, f32[8,1,128]{2,1,0:T(1,128)S(1)}, u32[]{:S(2)}, u32[]{:S(2)}) collective-permute-start(f32[8,1,128]{2,1,0:T(1,128)S(1)} %get-tuple-element.463), channel_id=1, source_target_pairs={{16,0},{32,16},{48,32},{64,48},{80,64},{96,80},{112,96},{128,112},... | collective-permute-start | bytes 12296 | tf_op jit(solution)/shard_map/ppermute | solution.py:20
  163.3 6.0 %collective-permute-start.27 = (f32[8,18,1]{2,1,0:T(8,128)S(1)}, f32[8,18,1]{2,1,0:T(8,128)S(1)}, u32[]{:S(2)}, u32[]{:S(2)}) collective-permute-start(f32[8,18,1]{2,1,0:T(8,128)S(1)} %get-tuple-element.443), channel_id=1, source_target_pairs={{1,0},{2,1},{3,2},{4,3},{5,4},{6,5},{7,6},{8,7},{9,8},{10,9},{11,1... | collective-permute-start | bytes 1736 | tf_op jit(solution)/shard_map/ppermute | solution.py:20
  180.2 9.2 %collective-permute-start.28 = (f32[8,1,130]{2,1,0:T(1,128)S(1)}, f32[8,1,130]{2,1,0:T(1,128)S(1)}, u32[]{:S(2)}, u32[]{:S(2)}) collective-permute-start(f32[8,1,130]{2,1,0:T(1,128)S(1)} %fusion.87), channel_id=1, source_target_pairs={{16,0},{32,16},{48,32},{64,48},{80,64},{96,80},{112,96},{128,112},... | collective-permute-start | bytes 12488 | tf_op jit(solution)/shard_map/ppermute | solution.py:30
  192.8 8.9 %collective-permute-done.29 = f32[8,1,130]{2,1,0:T(1,128)S(1)} collective-permute-done((f32[8,1,130]{2,1,0:T(1,128)S(1)}, f32[8,1,130]{2,1,0:T(1,128)S(1)}, u32[]{:S(2)}, u32[]{:S(2)}) %collective-permute-start.29) | collective-permute-done | bytes 4192 | tf_op jit(solution)/shard_map/ppermute | solution.py:30
  201.9 3.8 %collective-permute-start.30 = (f32[8,16,1]{2,1,0:T(8,128)S(1)}, f32[8,16,1]{2,1,0:T(8,128)S(1)}, u32[]{:S(2)}, u32[]{:S(2)}) collective-permute-start(f32[8,16,1]{2,1,0:T(8,128)S(1)} %get-tuple-element.401), channel_id=1, source_target_pairs={{1,0},{2,1},{3,2},{4,3},{5,4},{6,5},{7,6},{8,7},{9,8},{10,9},{11,1... | collective-permute-start | bytes 1544 | tf_op jit(solution)/shard_map/ppermute | solution.py:30
  206.8 2.1 collective-permute-start.31
  209.0 6.0 %collective-permute-done.31 = f32[8,16,1]{2,1,0:T(8,128)S(1)} collective-permute-done((f32[8,16,1]{2,1,0:T(8,128)S(1)}, f32[8,16,1]{2,1,0:T(8,128)S(1)}, u32[]{:S(2)}, u32[]{:S(2)}) %collective-permute-start.31) | collective-permute-done | bytes 544 | tf_op jit(solution)/shard_map/ppermute | solution.py:30
  219.9 2.4 collective-permute-start.33
  222.4 8.4 %collective-permute-done.33 = f32[4,1,130]{2,1,0:T(1,128)S(1)} collective-permute-done((f32[4,1,130]{2,1,0:T(1,128)S(1)}, f32[4,1,130]{2,1,0:T(1,128)S(1)}, u32[]{:S(2)}, u32[]{:S(2)}) %collective-permute-start.33) | collective-permute-done | bytes 2112 | tf_op jit(solution)/shard_map/ppermute | solution.py:30
  234.0 3.9 %collective-permute-start.35 = (f32[4,16,1]{2,1,0:T(8,128)S(1)}, f32[4,16,1]{2,1,0:T(8,128)S(1)}, u32[]{:S(2)}, u32[]{:S(2)}) collective-permute-start(f32[4,16,1]{2,1,0:T(8,128)S(1)} %get-tuple-element.438), channel_id=1, source_target_pairs={{0,1},{1,2},{2,3},{3,4},{4,5},{5,6},{6,7},{7,8},{8,9},{9,10},{10,1... | collective-permute-start | bytes 776 | tf_op jit(solution)/shard_map/ppermute | solution.py:30
  238.1 3.9 %collective-permute-done.35 = f32[4,16,1]{2,1,0:T(8,128)S(1)} collective-permute-done((f32[4,16,1]{2,1,0:T(8,128)S(1)}, f32[4,16,1]{2,1,0:T(8,128)S(1)}, u32[]{:S(2)}, u32[]{:S(2)}) %collective-permute-start.35) | collective-permute-done | bytes 288 | tf_op jit(solution)/shard_map/ppermute | solution.py:30
  246.6 2.6 collective-permute-start.37
  249.4 8.2 %collective-permute-done.37 = f32[4,1,130]{2,1,0:T(1,128)S(1)} collective-permute-done((f32[4,1,130]{2,1,0:T(1,128)S(1)}, f32[4,1,130]{2,1,0:T(1,128)S(1)}, u32[]{:S(2)}, u32[]{:S(2)}) %collective-permute-start.37) | collective-permute-done | bytes 2112 | tf_op jit(solution)/shard_map/ppermute | solution.py:30
  259.7 3.9 %collective-permute-start.39 = (f32[4,16,1]{2,1,0:T(8,128)S(1)}, f32[4,16,1]{2,1,0:T(8,128)S(1)}, u32[]{:S(2)}, u32[]{:S(2)}) collective-permute-start(f32[4,16,1]{2,1,0:T(8,128)S(1)} %get-tuple-element.434), channel_id=1, source_target_pairs={{0,1},{1,2},{2,3},{3,4},{4,5},{5,6},{6,7},{7,8},{8,9},{9,10},{10,1... | collective-permute-start | bytes 776 | tf_op jit(solution)/shard_map/ppermute | solution.py:30
  263.8 3.9 %collective-permute-done.39 = f32[4,16,1]{2,1,0:T(8,128)S(1)} collective-permute-done((f32[4,16,1]{2,1,0:T(8,128)S(1)}, f32[4,16,1]{2,1,0:T(8,128)S(1)}, u32[]{:S(2)}, u32[]{:S(2)}) %collective-permute-start.39) | collective-permute-done | bytes 288 | tf_op jit(solution)/shard_map/ppermute | solution.py:30
  275.7 9.0 %collective-permute-done.41 = f32[8,1,130]{2,1,0:T(1,128)S(1)} collective-permute-done((f32[8,1,130]{2,1,0:T(1,128)S(1)}, f32[8,1,130]{2,1,0:T(1,128)S(1)}, u32[]{:S(2)}, u32[]{:S(2)}) %collective-permute-start.41) | collective-permute-done | bytes 4192 | tf_op jit(solution)/shard_map/ppermute | solution.py:30
  286.9 3.9 %collective-permute-start.43 = (f32[8,16,1]{2,1,0:T(8,128)S(1)}, f32[8,16,1]{2,1,0:T(8,128)S(1)}, u32[]{:S(2)}, u32[]{:S(2)}) collective-permute-start(f32[8,16,1]{2,1,0:T(8,128)S(1)} %get-tuple-element.396), channel_id=1, source_target_pairs={{0,1},{1,2},{2,3},{3,4},{4,5},{5,6},{6,7},{7,8},{8,9},{9,10},{10,1... | collective-permute-start | bytes 1544 | tf_op jit(solution)/shard_map/ppermute | solution.py:30
  291.1 4.0 %collective-permute-done.43 = f32[8,16,1]{2,1,0:T(8,128)S(1)} collective-permute-done((f32[8,16,1]{2,1,0:T(8,128)S(1)}, f32[8,16,1]{2,1,0:T(8,128)S(1)}, u32[]{:S(2)}, u32[]{:S(2)}) %collective-permute-start.43) | collective-permute-done | bytes 544 | tf_op jit(solution)/shard_map/ppermute | solution.py:30
  298.4 2.4 collective-permute-start.45
  300.9 8.4 %collective-permute-done.45 = f32[4,1,130]{2,1,0:T(1,128)S(1)} collective-permute-done((f32[4,1,130]{2,1,0:T(1,128)S(1)}, f32[4,1,130]{2,1,0:T(1,128)S(1)}, u32[]{:S(2)}, u32[]{:S(2)}) %collective-permute-start.45) | collective-permute-done | bytes 2112 | tf_op jit(solution)/shard_map/ppermute | solution.py:30
  311.5 3.9 %collective-permute-start.47 = (f32[4,16,1]{2,1,0:T(8,128)S(1)}, f32[4,16,1]{2,1,0:T(8,128)S(1)}, u32[]{:S(2)}, u32[]{:S(2)}) collective-permute-start(f32[4,16,1]{2,1,0:T(8,128)S(1)} %get-tuple-element.430), channel_id=1, source_target_pairs={{0,1},{1,2},{2,3},{3,4},{4,5},{5,6},{6,7},{7,8},{8,9},{9,10},{10,1... | collective-permute-start | bytes 776 | tf_op jit(solution)/shard_map/ppermute | solution.py:30
  315.6 3.9 %collective-permute-done.47 = f32[4,16,1]{2,1,0:T(8,128)S(1)} collective-permute-done((f32[4,16,1]{2,1,0:T(8,128)S(1)}, f32[4,16,1]{2,1,0:T(8,128)S(1)}, u32[]{:S(2)}, u32[]{:S(2)}) %collective-permute-start.47) | collective-permute-done | bytes 288 | tf_op jit(solution)/shard_map/ppermute | solution.py:30
  320.7 2.2 fusion.2
  330.3 7.6 %collective-permute-done.49 = f32[36,1,130]{2,1,0:T(1,128)S(1)} collective-permute-done((f32[36,1,130]{2,1,0:T(1,128)S(1)}, f32[36,1,130]{2,1,0:T(1,128)S(1)}, u32[]{:S(2)}, u32[]{:S(2)}) %collective-permute-start.49) | collective-permute-done | bytes 18752 | tf_op jit(solution)/shard_map/ppermute | solution.py:30
  341.8 3.9 %collective-permute-start.51 = (f32[36,16,1]{2,1,0:T(8,128)S(1)}, f32[36,16,1]{2,1,0:T(8,128)S(1)}, u32[]{:S(2)}, u32[]{:S(2)}) collective-permute-start(f32[36,16,1]{2,1,0:T(8,128)S(1)} %get-tuple-element.379), channel_id=1, source_target_pairs={{0,1},{1,2},{2,3},{3,4},{4,5},{5,6},{6,7},{7,8},{8,9},{9,10},{10,1... | collective-permute-start | bytes 6920 | tf_op jit(solution)/shard_map/ppermute | solution.py:30
  345.8 2.6 collective-permute-done.50
  348.5 2.7 scatter-add.190
  352.7 4.9 %scatter-add.191 = f32[36,16,130]{2,1,0:T(8,128)S(1)} dynamic-update-slice(f32[36,16,130]{2,1,0:T(8,128)S(1)} %scatter-add.190, f32[36,16,1]{2,1,0:T(8,128)S(1)} %slice_add_fusion, s32[]{:T(128)} %constant.545.clone.1, s32[]{:T(128)} %constant.545.clone.1, s32[]{:T(128)} %constant.551.clone.1) | dynamic-update-slice | bytes 4612 | tf_op jit(solution)/shard_map/scatter-add | solution.py:174
  (442 shorter events, 107.6 us)
Async XLA Ops:
  11.9 34.7 %collective-permute-start.1 = (f32[48,1,128]{2,1,0:T(1,128)S(1)}, f32[48,1,128]{2,1,0:T(1,128)S(1)}, u32[]{:S(2)}, u32[]{:S(2)}) collective-permute-start(f32[48,1,128]{2,1,0:T(1,128)S(1)} %get-tuple-element.393), channel_id=1, source_target_pairs={{0,16},{16,32},{32,48},{48,64},{64,80},{80,96},{96,112},{112,128},... | collective-permute-start | bytes 73736 | tf_op jit(solution)/shard_map/ppermute | solution.py:18
  13.9 32.8 %collective-permute-start.4 = (f32[48,1,128]{2,1,0:T(1,128)S(1)}, f32[48,1,128]{2,1,0:T(1,128)S(1)}, u32[]{:S(2)}, u32[]{:S(2)}) collective-permute-start(f32[48,1,128]{2,1,0:T(1,128)S(1)} %get-tuple-element.392), channel_id=1, source_target_pairs={{16,0},{32,16},{48,32},{64,48},{80,64},{96,80},{112,96},{128,112},... | collective-permute-start | bytes 73736 | tf_op jit(solution)/shard_map/ppermute | solution.py:20
  26.5 4.8 %collective-permute-start = (f32[4,1,128]{2,1,0:T(1,128)S(1)}, f32[4,1,128]{2,1,0:T(1,128)S(1)}, u32[]{:S(2)}, u32[]{:S(2)}) collective-permute-start(f32[4,1,128]{2,1,0:T(1,128)S(1)} %get-tuple-element.524), channel_id=1, source_target_pairs={{16,0},{32,16},{48,32},{64,48},{80,64},{96,80},{112,96},{128,112},... | collective-permute-start | bytes 6152 | tf_op jit(solution)/shard_map/ppermute | solution.py:20
  29.1 11.0 %collective-permute-start.2 = (f32[4,1,128]{2,1,0:T(1,128)S(1)}, f32[4,1,128]{2,1,0:T(1,128)S(1)}, u32[]{:S(2)}, u32[]{:S(2)}) collective-permute-start(f32[4,1,128]{2,1,0:T(1,128)S(1)} %get-tuple-element.523), channel_id=1, source_target_pairs={{0,16},{16,32},{32,48},{48,64},{64,80},{80,96},{96,112},{112,128},... | collective-permute-start | bytes 6152 | tf_op jit(solution)/shard_map/ppermute | solution.py:18
  40.2 15.0 %collective-permute-start.3 = (f32[4,18,1]{2,1,0:T(8,128)S(1)}, f32[4,18,1]{2,1,0:T(8,128)S(1)}, u32[]{:S(2)}, u32[]{:S(2)}) collective-permute-start(f32[4,18,1]{2,1,0:T(8,128)S(1)} %get-tuple-element.482), channel_id=1, source_target_pairs={{1,0},{2,1},{3,2},{4,3},{5,4},{6,5},{7,6},{8,7},{9,8},{10,9},{11,1... | collective-permute-start | bytes 872 | tf_op jit(solution)/shard_map/ppermute | solution.py:20
  44.7 10.6 %collective-permute-start.6 = (f32[4,18,1]{2,1,0:T(8,128)S(1)}, f32[4,18,1]{2,1,0:T(8,128)S(1)}, u32[]{:S(2)}, u32[]{:S(2)}) collective-permute-start(f32[4,18,1]{2,1,0:T(8,128)S(1)} %get-tuple-element.483), channel_id=1, source_target_pairs={{0,1},{1,2},{2,3},{3,4},{4,5},{5,6},{6,7},{7,8},{8,9},{9,10},{10,1... | collective-permute-start | bytes 872 | tf_op jit(solution)/shard_map/ppermute | solution.py:18
  47.3 7.7 %collective-permute-start.5 = (f32[48,18,1]{0,1,2:T(8,128)S(1)}, f32[48,18,1]{0,1,2:T(8,128)S(1)}, u32[]{:S(2)}, u32[]{:S(2)}) collective-permute-start(f32[48,18,1]{0,1,2:T(8,128)S(1)} %copy.62), channel_id=1, source_target_pairs={{0,1},{1,2},{2,3},{3,4},{4,5},{5,6},{6,7},{7,8},{8,9},{9,10},{10,1... | collective-permute-start | bytes 10376 | tf_op jit(solution)/shard_map/ppermute | solution.py:18
  56.1 8.7 %collective-permute-start.7 = (f32[4,1,128]{2,1,0:T(1,128)S(1)}, f32[4,1,128]{2,1,0:T(1,128)S(1)}, u32[]{:S(2)}, u32[]{:S(2)}) collective-permute-start(f32[4,1,128]{2,1,0:T(1,128)S(1)} %get-tuple-element.520), channel_id=1, source_target_pairs={{16,0},{32,16},{48,32},{64,48},{80,64},{96,80},{112,96},{128,112},... | collective-permute-start | bytes 6152 | tf_op jit(solution)/shard_map/ppermute | solution.py:20
  58.2 10.9 %collective-permute-start.8 = (f32[4,1,128]{2,1,0:T(1,128)S(1)}, f32[4,1,128]{2,1,0:T(1,128)S(1)}, u32[]{:S(2)}, u32[]{:S(2)}) collective-permute-start(f32[4,1,128]{2,1,0:T(1,128)S(1)} %get-tuple-element.519), channel_id=1, source_target_pairs={{0,16},{16,32},{32,48},{48,64},{64,80},{80,96},{96,112},{112,128},... | collective-permute-start | bytes 6152 | tf_op jit(solution)/shard_map/ppermute | solution.py:18
  60.8 16.3 %collective-permute-start.23 = (f32[48,18,1]{0,1,2:T(8,128)S(1)}, f32[48,18,1]{0,1,2:T(8,128)S(1)}, u32[]{:S(2)}, u32[]{:S(2)}) collective-permute-start(f32[48,18,1]{0,1,2:T(8,128)S(1)} %copy.64), channel_id=1, source_target_pairs={{1,0},{2,1},{3,2},{4,3},{5,4},{6,5},{7,6},{8,7},{9,8},{10,9},{11,1... | collective-permute-start | bytes 10376 | tf_op jit(solution)/shard_map/ppermute | solution.py:20
  69.2 8.3 %collective-permute-start.10 = (f32[4,18,1]{2,1,0:T(8,128)S(1)}, f32[4,18,1]{2,1,0:T(8,128)S(1)}, u32[]{:S(2)}, u32[]{:S(2)}) collective-permute-start(f32[4,18,1]{2,1,0:T(8,128)S(1)} %get-tuple-element.481), channel_id=1, source_target_pairs={{0,1},{1,2},{2,3},{3,4},{4,5},{5,6},{6,7},{7,8},{8,9},{9,10},{10,1... | collective-permute-start | bytes 872 | tf_op jit(solution)/shard_map/ppermute | solution.py:18
  71.1 7.8 %collective-permute-start.9 = (f32[4,18,1]{2,1,0:T(8,128)S(1)}, f32[4,18,1]{2,1,0:T(8,128)S(1)}, u32[]{:S(2)}, u32[]{:S(2)}) collective-permute-start(f32[4,18,1]{2,1,0:T(8,128)S(1)} %get-tuple-element.480), channel_id=1, source_target_pairs={{1,0},{2,1},{3,2},{4,3},{5,4},{6,5},{7,6},{8,7},{9,8},{10,9},{11,1... | collective-permute-start | bytes 872 | tf_op jit(solution)/shard_map/ppermute | solution.py:20
  79.6 17.0 %collective-permute-start.11 = (f32[4,1,128]{2,1,0:T(1,128)S(1)}, f32[4,1,128]{2,1,0:T(1,128)S(1)}, u32[]{:S(2)}, u32[]{:S(2)}) collective-permute-start(f32[4,1,128]{2,1,0:T(1,128)S(1)} %get-tuple-element.514), channel_id=1, source_target_pairs={{16,0},{32,16},{48,32},{64,48},{80,64},{96,80},{112,96},{128,112},... | collective-permute-start | bytes 6152 | tf_op jit(solution)/shard_map/ppermute | solution.py:20
  83.1 13.6 %collective-permute-start.12 = (f32[4,1,128]{2,1,0:T(1,128)S(1)}, f32[4,1,128]{2,1,0:T(1,128)S(1)}, u32[]{:S(2)}, u32[]{:S(2)}) collective-permute-start(f32[4,1,128]{2,1,0:T(1,128)S(1)} %get-tuple-element.513), channel_id=1, source_target_pairs={{0,16},{16,32},{32,48},{48,64},{64,80},{80,96},{96,112},{112,128},... | collective-permute-start | bytes 6152 | tf_op jit(solution)/shard_map/ppermute | solution.py:18
  85.1 11.7 %collective-permute-start.19 = (f32[8,1,128]{2,1,0:T(1,128)S(1)}, f32[8,1,128]{2,1,0:T(1,128)S(1)}, u32[]{:S(2)}, u32[]{:S(2)}) collective-permute-start(f32[8,1,128]{2,1,0:T(1,128)S(1)} %get-tuple-element.464), channel_id=1, source_target_pairs={{0,16},{16,32},{32,48},{48,64},{64,80},{80,96},{96,112},{112,128},... | collective-permute-start | bytes 12296 | tf_op jit(solution)/shard_map/ppermute | solution.py:18
  87.0 11.0 %collective-permute-start.20 = (f32[8,1,128]{2,1,0:T(1,128)S(1)}, f32[8,1,128]{2,1,0:T(1,128)S(1)}, u32[]{:S(2)}, u32[]{:S(2)}) collective-permute-start(f32[8,1,128]{2,1,0:T(1,128)S(1)} %get-tuple-element.465), channel_id=1, source_target_pairs={{16,0},{32,16},{48,32},{64,48},{80,64},{96,80},{112,96},{128,112},... | collective-permute-start | bytes 12296 | tf_op jit(solution)/shard_map/ppermute | solution.py:20
  98.1 14.0 %collective-permute-start.21 = (f32[8,18,1]{2,1,0:T(8,128)S(1)}, f32[8,18,1]{2,1,0:T(8,128)S(1)}, u32[]{:S(2)}, u32[]{:S(2)}) collective-permute-start(f32[8,18,1]{2,1,0:T(8,128)S(1)} %get-tuple-element.444), channel_id=1, source_target_pairs={{0,1},{1,2},{2,3},{3,4},{4,5},{5,6},{6,7},{7,8},{8,9},{9,10},{10,1... | collective-permute-start | bytes 1736 | tf_op jit(solution)/shard_map/ppermute | solution.py:18
  100.0 12.0 %collective-permute-start.22 = (f32[8,18,1]{2,1,0:T(8,128)S(1)}, f32[8,18,1]{2,1,0:T(8,128)S(1)}, u32[]{:S(2)}, u32[]{:S(2)}) collective-permute-start(f32[8,18,1]{2,1,0:T(8,128)S(1)} %get-tuple-element.445), channel_id=1, source_target_pairs={{1,0},{2,1},{3,2},{4,3},{5,4},{6,5},{7,6},{8,7},{9,8},{10,9},{11,1... | collective-permute-start | bytes 1736 | tf_op jit(solution)/shard_map/ppermute | solution.py:20
  106.2 6.8 %collective-permute-start.13 = (f32[4,18,1]{2,1,0:T(8,128)S(1)}, f32[4,18,1]{2,1,0:T(8,128)S(1)}, u32[]{:S(2)}, u32[]{:S(2)}) collective-permute-start(f32[4,18,1]{2,1,0:T(8,128)S(1)} %get-tuple-element.478), channel_id=1, source_target_pairs={{1,0},{2,1},{3,2},{4,3},{5,4},{6,5},{7,6},{8,7},{9,8},{10,9},{11,1... | collective-permute-start | bytes 872 | tf_op jit(solution)/shard_map/ppermute | solution.py:20
  110.1 8.1 %collective-permute-start.14 = (f32[4,18,1]{2,1,0:T(8,128)S(1)}, f32[4,18,1]{2,1,0:T(8,128)S(1)}, u32[]{:S(2)}, u32[]{:S(2)}) collective-permute-start(f32[4,18,1]{2,1,0:T(8,128)S(1)} %get-tuple-element.479), channel_id=1, source_target_pairs={{0,1},{1,2},{2,3},{3,4},{4,5},{5,6},{6,7},{7,8},{8,9},{9,10},{10,1... | collective-permute-start | bytes 872 | tf_op jit(solution)/shard_map/ppermute | solution.py:18
  118.9 11.5 %collective-permute-start.15 = (f32[4,1,128]{2,1,0:T(1,128)S(1)}, f32[4,1,128]{2,1,0:T(1,128)S(1)}, u32[]{:S(2)}, u32[]{:S(2)}) collective-permute-start(f32[4,1,128]{2,1,0:T(1,128)S(1)} %get-tuple-element.510), channel_id=1, source_target_pairs={{16,0},{32,16},{48,32},{64,48},{80,64},{96,80},{112,96},{128,112},... | collective-permute-start | bytes 6152 | tf_op jit(solution)/shard_map/ppermute | solution.py:20
  126.6 10.9 %collective-permute-start.16 = (f32[4,1,128]{2,1,0:T(1,128)S(1)}, f32[4,1,128]{2,1,0:T(1,128)S(1)}, u32[]{:S(2)}, u32[]{:S(2)}) collective-permute-start(f32[4,1,128]{2,1,0:T(1,128)S(1)} %get-tuple-element.509), channel_id=1, source_target_pairs={{0,16},{16,32},{32,48},{48,64},{64,80},{80,96},{96,112},{112,128},... | collective-permute-start | bytes 6152 | tf_op jit(solution)/shard_map/ppermute | solution.py:18
  137.6 6.0 %collective-permute-start.17 = (f32[4,18,1]{2,1,0:T(8,128)S(1)}, f32[4,18,1]{2,1,0:T(8,128)S(1)}, u32[]{:S(2)}, u32[]{:S(2)}) collective-permute-start(f32[4,18,1]{2,1,0:T(8,128)S(1)} %get-tuple-element.476), channel_id=1, source_target_pairs={{1,0},{2,1},{3,2},{4,3},{5,4},{6,5},{7,6},{8,7},{9,8},{10,9},{11,1... | collective-permute-start | bytes 872 | tf_op jit(solution)/shard_map/ppermute | solution.py:20
  139.5 8.1 %collective-permute-start.18 = (f32[4,18,1]{2,1,0:T(8,128)S(1)}, f32[4,18,1]{2,1,0:T(8,128)S(1)}, u32[]{:S(2)}, u32[]{:S(2)}) collective-permute-start(f32[4,18,1]{2,1,0:T(8,128)S(1)} %get-tuple-element.477), channel_id=1, source_target_pairs={{0,1},{1,2},{2,3},{3,4},{4,5},{5,6},{6,7},{7,8},{8,9},{9,10},{10,1... | collective-permute-start | bytes 872 | tf_op jit(solution)/shard_map/ppermute | solution.py:18
  148.3 11.6 %collective-permute-start.24 = (f32[8,1,128]{2,1,0:T(1,128)S(1)}, f32[8,1,128]{2,1,0:T(1,128)S(1)}, u32[]{:S(2)}, u32[]{:S(2)}) collective-permute-start(f32[8,1,128]{2,1,0:T(1,128)S(1)} %get-tuple-element.462), channel_id=1, source_target_pairs={{0,16},{16,32},{32,48},{48,64},{64,80},{80,96},{96,112},{112,128},... | collective-permute-start | bytes 12296 | tf_op jit(solution)/shard_map/ppermute | solution.py:18
  150.3 11.0 %collective-permute-start.25 = (f32[8,1,128]{2,1,0:T(1,128)S(1)}, f32[8,1,128]{2,1,0:T(1,128)S(1)}, u32[]{:S(2)}, u32[]{:S(2)}) collective-permute-start(f32[8,1,128]{2,1,0:T(1,128)S(1)} %get-tuple-element.463), channel_id=1, source_target_pairs={{16,0},{32,16},{48,32},{64,48},{80,64},{96,80},{112,96},{128,112},... | collective-permute-start | bytes 12296 | tf_op jit(solution)/shard_map/ppermute | solution.py:20
  161.4 11.9 %collective-permute-start.26 = (f32[8,18,1]{2,1,0:T(8,128)S(1)}, f32[8,18,1]{2,1,0:T(8,128)S(1)}, u32[]{:S(2)}, u32[]{:S(2)}) collective-permute-start(f32[8,18,1]{2,1,0:T(8,128)S(1)} %get-tuple-element.442), channel_id=1, source_target_pairs={{0,1},{1,2},{2,3},{3,4},{4,5},{5,6},{6,7},{7,8},{8,9},{9,10},{10,1... | collective-permute-start | bytes 1736 | tf_op jit(solution)/shard_map/ppermute | solution.py:18
  163.3 10.0 %collective-permute-start.27 = (f32[8,18,1]{2,1,0:T(8,128)S(1)}, f32[8,18,1]{2,1,0:T(8,128)S(1)}, u32[]{:S(2)}, u32[]{:S(2)}) collective-permute-start(f32[8,18,1]{2,1,0:T(8,128)S(1)} %get-tuple-element.443), channel_id=1, source_target_pairs={{1,0},{2,1},{3,2},{4,3},{5,4},{6,5},{7,6},{8,7},{9,8},{10,9},{11,1... | collective-permute-start | bytes 1736 | tf_op jit(solution)/shard_map/ppermute | solution.py:20
  180.2 10.5 %collective-permute-start.28 = (f32[8,1,130]{2,1,0:T(1,128)S(1)}, f32[8,1,130]{2,1,0:T(1,128)S(1)}, u32[]{:S(2)}, u32[]{:S(2)}) collective-permute-start(f32[8,1,130]{2,1,0:T(1,128)S(1)} %fusion.87), channel_id=1, source_target_pairs={{16,0},{32,16},{48,32},{64,48},{80,64},{96,80},{112,96},{128,112},... | collective-permute-start | bytes 12488 | tf_op jit(solution)/shard_map/ppermute | solution.py:30
  190.7 11.0 %collective-permute-start.29 = (f32[8,1,130]{2,1,0:T(1,128)S(1)}, f32[8,1,130]{2,1,0:T(1,128)S(1)}, u32[]{:S(2)}, u32[]{:S(2)}) collective-permute-start(f32[8,1,130]{2,1,0:T(1,128)S(1)} %get-tuple-element.402), channel_id=1, source_target_pairs={{0,16},{16,32},{32,48},{48,64},{64,80},{80,96},{96,112},{112,128},... | collective-permute-start | bytes 12488 | tf_op jit(solution)/shard_map/ppermute | solution.py:30
  201.9 7.0 %collective-permute-start.30 = (f32[8,16,1]{2,1,0:T(8,128)S(1)}, f32[8,16,1]{2,1,0:T(8,128)S(1)}, u32[]{:S(2)}, u32[]{:S(2)}) collective-permute-start(f32[8,16,1]{2,1,0:T(8,128)S(1)} %get-tuple-element.401), channel_id=1, source_target_pairs={{1,0},{2,1},{3,2},{4,3},{5,4},{6,5},{7,6},{8,7},{9,8},{10,9},{11,1... | collective-permute-start | bytes 1544 | tf_op jit(solution)/shard_map/ppermute | solution.py:30
  206.8 8.3 %collective-permute-start.31 = (f32[8,16,1]{2,1,0:T(8,128)S(1)}, f32[8,16,1]{2,1,0:T(8,128)S(1)}, u32[]{:S(2)}, u32[]{:S(2)}) collective-permute-start(f32[8,16,1]{2,1,0:T(8,128)S(1)} %get-tuple-element.400), channel_id=1, source_target_pairs={{0,1},{1,2},{2,3},{3,4},{4,5},{5,6},{6,7},{7,8},{8,9},{9,10},{10,1... | collective-permute-start | bytes 1544 | tf_op jit(solution)/shard_map/ppermute | solution.py:30
  216.9 5.4 %collective-permute-start.32 = (f32[4,1,130]{2,1,0:T(1,128)S(1)}, f32[4,1,130]{2,1,0:T(1,128)S(1)}, u32[]{:S(2)}, u32[]{:S(2)}) collective-permute-start(f32[4,1,130]{2,1,0:T(1,128)S(1)} %get-tuple-element.441), channel_id=1, source_target_pairs={{16,0},{32,16},{48,32},{64,48},{80,64},{96,80},{112,96},{128,112},... | collective-permute-start | bytes 6248 | tf_op jit(solution)/shard_map/ppermute | solution.py:30
  219.9 10.9 %collective-permute-start.33 = (f32[4,1,130]{2,1,0:T(1,128)S(1)}, f32[4,1,130]{2,1,0:T(1,128)S(1)}, u32[]{:S(2)}, u32[]{:S(2)}) collective-permute-start(f32[4,1,130]{2,1,0:T(1,128)S(1)} %get-tuple-element.440), channel_id=1, source_target_pairs={{0,16},{16,32},{32,48},{48,64},{64,80},{80,96},{96,112},{112,128},... | collective-permute-start | bytes 6248 | tf_op jit(solution)/shard_map/ppermute | solution.py:30
  231.0 6.9 %collective-permute-start.34 = (f32[4,16,1]{2,1,0:T(8,128)S(1)}, f32[4,16,1]{2,1,0:T(8,128)S(1)}, u32[]{:S(2)}, u32[]{:S(2)}) collective-permute-start(f32[4,16,1]{2,1,0:T(8,128)S(1)} %get-tuple-element.439), channel_id=1, source_target_pairs={{1,0},{2,1},{3,2},{4,3},{5,4},{6,5},{7,6},{8,7},{9,8},{10,9},{11,1... | collective-permute-start | bytes 776 | tf_op jit(solution)/shard_map/ppermute | solution.py:30
  234.0 7.9 %collective-permute-start.35 = (f32[4,16,1]{2,1,0:T(8,128)S(1)}, f32[4,16,1]{2,1,0:T(8,128)S(1)}, u32[]{:S(2)}, u32[]{:S(2)}) collective-permute-start(f32[4,16,1]{2,1,0:T(8,128)S(1)} %get-tuple-element.438), channel_id=1, source_target_pairs={{0,1},{1,2},{2,3},{3,4},{4,5},{5,6},{6,7},{7,8},{8,9},{9,10},{10,1... | collective-permute-start | bytes 776 | tf_op jit(solution)/shard_map/ppermute | solution.py:30
  246.6 10.9 %collective-permute-start.37 = (f32[4,1,130]{2,1,0:T(1,128)S(1)}, f32[4,1,130]{2,1,0:T(1,128)S(1)}, u32[]{:S(2)}, u32[]{:S(2)}) collective-permute-start(f32[4,1,130]{2,1,0:T(1,128)S(1)} %get-tuple-element.436), channel_id=1, source_target_pairs={{0,16},{16,32},{32,48},{48,64},{64,80},{80,96},{96,112},{112,128},... | collective-permute-start | bytes 6248 | tf_op jit(solution)/shard_map/ppermute | solution.py:30
  257.7 6.0 %collective-permute-start.38 = (f32[4,16,1]{2,1,0:T(8,128)S(1)}, f32[4,16,1]{2,1,0:T(8,128)S(1)}, u32[]{:S(2)}, u32[]{:S(2)}) collective-permute-start(f32[4,16,1]{2,1,0:T(8,128)S(1)} %get-tuple-element.435), channel_id=1, source_target_pairs={{1,0},{2,1},{3,2},{4,3},{5,4},{6,5},{7,6},{8,7},{9,8},{10,9},{11,1... | collective-permute-start | bytes 776 | tf_op jit(solution)/shard_map/ppermute | solution.py:30
  259.7 7.9 %collective-permute-start.39 = (f32[4,16,1]{2,1,0:T(8,128)S(1)}, f32[4,16,1]{2,1,0:T(8,128)S(1)}, u32[]{:S(2)}, u32[]{:S(2)}) collective-permute-start(f32[4,16,1]{2,1,0:T(8,128)S(1)} %get-tuple-element.434), channel_id=1, source_target_pairs={{0,1},{1,2},{2,3},{3,4},{4,5},{5,6},{6,7},{7,8},{8,9},{9,10},{10,1... | collective-permute-start | bytes 776 | tf_op jit(solution)/shard_map/ppermute | solution.py:30
  273.7 11.0 %collective-permute-start.41 = (f32[8,1,130]{2,1,0:T(1,128)S(1)}, f32[8,1,130]{2,1,0:T(1,128)S(1)}, u32[]{:S(2)}, u32[]{:S(2)}) collective-permute-start(f32[8,1,130]{2,1,0:T(1,128)S(1)} %get-tuple-element.398), channel_id=1, source_target_pairs={{0,16},{16,32},{32,48},{48,64},{64,80},{80,96},{96,112},{112,128},... | collective-permute-start | bytes 12488 | tf_op jit(solution)/shard_map/ppermute | solution.py:30
  284.8 6.2 %collective-permute-start.42 = (f32[8,16,1]{2,1,0:T(8,128)S(1)}, f32[8,16,1]{2,1,0:T(8,128)S(1)}, u32[]{:S(2)}, u32[]{:S(2)}) collective-permute-start(f32[8,16,1]{2,1,0:T(8,128)S(1)} %get-tuple-element.397), channel_id=1, source_target_pairs={{1,0},{2,1},{3,2},{4,3},{5,4},{6,5},{7,6},{8,7},{9,8},{10,9},{11,1... | collective-permute-start | bytes 1544 | tf_op jit(solution)/shard_map/ppermute | solution.py:30
  286.9 8.3 %collective-permute-start.43 = (f32[8,16,1]{2,1,0:T(8,128)S(1)}, f32[8,16,1]{2,1,0:T(8,128)S(1)}, u32[]{:S(2)}, u32[]{:S(2)}) collective-permute-start(f32[8,16,1]{2,1,0:T(8,128)S(1)} %get-tuple-element.396), channel_id=1, source_target_pairs={{0,1},{1,2},{2,3},{3,4},{4,5},{5,6},{6,7},{7,8},{8,9},{9,10},{10,1... | collective-permute-start | bytes 1544 | tf_op jit(solution)/shard_map/ppermute | solution.py:30
  298.4 10.9 %collective-permute-start.45 = (f32[4,1,130]{2,1,0:T(1,128)S(1)}, f32[4,1,130]{2,1,0:T(1,128)S(1)}, u32[]{:S(2)}, u32[]{:S(2)}) collective-permute-start(f32[4,1,130]{2,1,0:T(1,128)S(1)} %get-tuple-element.432), channel_id=1, source_target_pairs={{0,16},{16,32},{32,48},{48,64},{64,80},{80,96},{96,112},{112,128},... | collective-permute-start | bytes 6248 | tf_op jit(solution)/shard_map/ppermute | solution.py:30
  309.5 6.0 %collective-permute-start.46 = (f32[4,16,1]{2,1,0:T(8,128)S(1)}, f32[4,16,1]{2,1,0:T(8,128)S(1)}, u32[]{:S(2)}, u32[]{:S(2)}) collective-permute-start(f32[4,16,1]{2,1,0:T(8,128)S(1)} %get-tuple-element.431), channel_id=1, source_target_pairs={{1,0},{2,1},{3,2},{4,3},{5,4},{6,5},{7,6},{8,7},{9,8},{10,9},{11,1... | collective-permute-start | bytes 776 | tf_op jit(solution)/shard_map/ppermute | solution.py:30
  311.5 7.9 %collective-permute-start.47 = (f32[4,16,1]{2,1,0:T(8,128)S(1)}, f32[4,16,1]{2,1,0:T(8,128)S(1)}, u32[]{:S(2)}, u32[]{:S(2)}) collective-permute-start(f32[4,16,1]{2,1,0:T(8,128)S(1)} %get-tuple-element.430), channel_id=1, source_target_pairs={{0,1},{1,2},{2,3},{3,4},{4,5},{5,6},{6,7},{7,8},{8,9},{9,10},{10,1... | collective-permute-start | bytes 776 | tf_op jit(solution)/shard_map/ppermute | solution.py:30
  326.6 11.3 %collective-permute-start.49 = (f32[36,1,130]{2,1,0:T(1,128)S(1)}, f32[36,1,130]{2,1,0:T(1,128)S(1)}, u32[]{:S(2)}, u32[]{:S(2)}) collective-permute-start(f32[36,1,130]{2,1,0:T(1,128)S(1)} %get-tuple-element.381), channel_id=1, source_target_pairs={{0,16},{16,32},{32,48},{48,64},{64,80},{80,96},{96,112},{112,128},... | collective-permute-start | bytes 56168 | tf_op jit(solution)/shard_map/ppermute | solution.py:30
  339.8 8.6 %collective-permute-start.50 = (f32[36,16,1]{2,1,0:T(8,128)S(1)}, f32[36,16,1]{2,1,0:T(8,128)S(1)}, u32[]{:S(2)}, u32[]{:S(2)}) collective-permute-start(f32[36,16,1]{2,1,0:T(8,128)S(1)} %get-tuple-element.380), channel_id=1, source_target_pairs={{1,0},{2,1},{3,2},{4,3},{5,4},{6,5},{7,6},{8,7},{9,8},{10,9},{11,1... | collective-permute-start | bytes 6920 | tf_op jit(solution)/shard_map/ppermute | solution.py:30
  341.8 10.7 %collective-permute-start.51 = (f32[36,16,1]{2,1,0:T(8,128)S(1)}, f32[36,16,1]{2,1,0:T(8,128)S(1)}, u32[]{:S(2)}, u32[]{:S(2)}) collective-permute-start(f32[36,16,1]{2,1,0:T(8,128)S(1)} %get-tuple-element.379), channel_id=1, source_target_pairs={{0,1},{1,2},{2,3},{3,4},{4,5},{5,6},{6,7},{7,8},{8,9},{9,10},{10,1... | collective-permute-start | bytes 6920 | tf_op jit(solution)/shard_map/ppermute | solution.py:30
  (94 other events, 1989.1 us)
where the time goes:
time: 362 us; the launch traced here: 359 us
  starting transfers between devices  177 us (49%)
  waiting for transfers between devices  119 us (33%)
  other arithmetic  35.6 us (10%)
  local copies, waits for them, and re-layouts  24.1 us (7%)
    ppermute x24, waiting for transfers between devices, shifted(): return lax.ppermute(value, axis, pairs)  80.6 us
    ppermute x14, starting transfers between devices, extended(): lax.ppermute(head, axis, [((i + 1) % count, i) for i in range(ends)])  80 us
    ppermute x24, starting transfers between devices, shifted(): return lax.ppermute(value, axis, pairs)  67 us
    ppermute x14, waiting for transfers between devices, extended(): lax.ppermute(tail, axis, [(i, (i + 1) % count) for i in range(ends)])  34.3 us
    ppermute x14, starting transfers between devices, extended(): lax.ppermute(tail, axis, [(i, (i + 1) % count) for i in range(ends)])  30.2 us
  transfers between devices with their start and end apart: 52, of which 27 were waited for; matrix products, arithmetic and copies ran while one was open for 5% of the time, Pallas kernels for 0%

commit v1 on v0

v1 whole, which is shorter than its diff:
```python
import jax
import jax.numpy as jnp
from jax import lax
from jax.experimental import pallas as pl
from jax.experimental.pallas import tpu as pltpu
from jax.sharding import PartitionSpec as P

MESH = pl.DeviceIdType.MESH
time_step = 0.05

P0, S0, TX, TY, TZ, PV, UP, SLOTS = 0, 4, 8, 12, 16, 19, 23, 27
GROUPS = 4
WELLS = 64


def exchange_kernel(
    p0, s0, tx, ty, tz, pv, up, cell, rate, plan, observed,
    own, own_list, from_n, from_s, ext_n, ext_s, from_e, from_w, from_ne, from_nw, from_se, from_sw,
    up_int, cell_v, rate_v, plan_v, obs_v, xtra_n, xtra_s, pack_e, pack_w, in_sem, send_sem, recv_sem,
):
    gx, gy = lax.axis_index("gx"), lax.axis_index("gy")
    nx, ny = lax.axis_size("gx"), lax.axis_size("gy")
    north, south = lax.rem(gx + nx - 1, nx), lax.rem(gx + 1, nx)
    west, east = lax.rem(gy + ny - 1, ny), lax.rem(gy + 1, ny)

    barrier = pltpu.get_barrier_semaphore()
    for peer in (
        (north, gy), (south, gy), (gx, east), (gx, west),
        (south, east), (south, west), (north, east), (north, west),
    ):
        pl.semaphore_signal(barrier, inc=1, device_id=peer, device_id_type=MESH)

    loads = [
        (p0, own.at[pl.ds(P0, 4)]),
        (s0, own.at[pl.ds(S0, 4)]),
        (tx, own.at[pl.ds(TX, 4)]),
        (ty, own.at[pl.ds(TY, 4)]),
        (tz, own.at[pl.ds(TZ, 3)]),
        (pv, own.at[pl.ds(PV, 4)]),
        (up, up_int),
        (cell, cell_v),
        (rate, rate_v),
        (plan, plan_v),
        (observed, obs_v),
    ]
    loads = [pltpu.make_async_copy(a, b, in_sem.at[i]) for i, (a, b) in enumerate(loads)]
    for load in loads:
        load.start()
    for load in loads:
        load.wait()

    own[UP:SLOTS] = up_int[...].astype(jnp.float32)

    rates = rate_v[0] * 0.5
    rows = [
        cell_v[0].astype(jnp.float32),
        rates * plan_v[0, 0].astype(jnp.float32),
        rates * plan_v[1, 0].astype(jnp.float32),
        obs_v[0, 0, 0],
        obs_v[0, 1, 0],
        obs_v[1, 0, 0],
        obs_v[1, 1, 0],
        jnp.zeros((1, WELLS), jnp.float32),
    ]
    wells = jnp.concatenate(rows, axis=0)
    wells = jnp.concatenate([wells, wells], axis=1)
    own_list[...] = wells

    for layer in range(4):
        xtra_s[0, layer : layer + 1] = own[P0 + layer, 8:9]
        xtra_s[0, 4 + layer : 5 + layer] = own[TY + layer, 8:9]
        xtra_s[1, layer : layer + 1] = own[P0 + layer, 7:8]
        xtra_s[1, 4 + layer : 5 + layer] = own[P0 + layer, 9:10]
        xtra_s[2, layer : layer + 1] = own[TX + layer, 7:8]
        xtra_s[2, 4 + layer : 5 + layer] = own[TX + layer, 8:9]
        xtra_s[3, layer : layer + 1] = own[PV + layer, 8:9]
        if layer < 3:
            xtra_s[3, 4 + layer : 5 + layer] = own[TZ + layer, 8:9]
        xtra_n[0, layer : layer + 1] = own[P0 + layer, 7:8]
        xtra_n[0, 4 + layer : 5 + layer] = own[TX + layer, 7:8]
    xtra_s[3, 7:8] = jnp.zeros((1, 128), jnp.float32)
    xtra_s[4] = wells
    xtra_n[1] = wells

    block = lax.broadcasted_iota(jnp.int32, (8, 128), 1) // 16
    for pack in (pack_e, pack_w):
        pack[0] = xtra_s[0]
        pack[1] = wells
        pack[10] = wells
    for half in range(2):
        for group in range(GROUPS):
            first = second = None
            for k in range(min(8, SLOTS - 8 * group)):
                tile = own[8 * group + k, 8 * half : 8 * half + 8]
                if k:
                    tile = pltpu.roll(tile, 16 * k, axis=1)
                first = tile if first is None else jnp.where(block == k, tile, first)
                second = tile if second is None else jnp.where(block == (k + 7) % 8, tile, second)
            pack_e[2 + 4 * half + group] = first
            pack_w[2 + 4 * half + group] = second

    pl.semaphore_wait(barrier, 8)

    sends = [
        (own.at[:, pl.ds(0, 8), :], from_s, (north, gy)),
        (own.at[:, pl.ds(8, 8), :], from_n, (south, gy)),
        (xtra_s, ext_s, (north, gy)),
        (xtra_n, ext_n, (south, gy)),
        (pack_w.at[pl.ds(1, 9)], from_w, (gx, east)),
        (pack_e.at[pl.ds(1, 9)], from_e, (gx, west)),
        (pack_w.at[pl.ds(6, 5)], from_nw, (south, east)),
        (pack_e.at[pl.ds(6, 5)], from_ne, (south, west)),
        (pack_w.at[pl.ds(0, 6)], from_sw, (north, east)),
        (pack_e.at[pl.ds(0, 6)], from_se, (north, west)),
    ]
    sends = [
        pltpu.make_async_remote_copy(
            src_ref=src, dst_ref=dst, send_sem=send_sem.at[i], recv_sem=recv_sem.at[i],
            device_id=peer, device_id_type=MESH,
        )
        for i, (src, dst, peer) in enumerate(sends)
    ]
    for send in sends:
        send.start()
    for send in sends:
        send.wait()


def exchange(*args):
    f32 = jnp.float32
    tile = lambda *lead: jax.ShapeDtypeStruct(lead + (8, 128), f32)
    outs = (
        jax.ShapeDtypeStruct((SLOTS, 16, 128), f32),
        tile(),
        tile(SLOTS), tile(SLOTS), tile(2), tile(5),
        tile(9), tile(9),
        tile(5), tile(5), tile(6), tile(6),
    )
    return pl.pallas_call(
        exchange_kernel,
        out_shape=outs,
        in_specs=[pl.BlockSpec(memory_space=pl.ANY)] * 11,
        out_specs=[pl.BlockSpec(memory_space=pltpu.VMEM)] * 12,
        scratch_shapes=[
            pltpu.VMEM((4, 16, 128), jnp.int32),
            pltpu.VMEM((1, 1, WELLS), jnp.int32),
            pltpu.VMEM((1, 1, WELLS), f32),
            pltpu.VMEM((2, 1, 1, WELLS), jnp.int32),
            pltpu.VMEM((2, 2, 1, 1, WELLS), f32),
            pltpu.VMEM((2, 8, 128), f32),
            pltpu.VMEM((5, 8, 128), f32),
            pltpu.VMEM((11, 8, 128), f32),
            pltpu.VMEM((11, 8, 128), f32),
            pltpu.SemaphoreType.DMA((11,)),
            pltpu.SemaphoreType.DMA((10,)),
            pltpu.SemaphoreType.DMA((10,)),
        ],
        compiler_params=pltpu.CompilerParams(collective_id=0, has_side_effects=True),
    )(*args)


def x_next(v):
    return pltpu.roll(v, v.shape[0] - 1, axis=0)


def x_prev(v):
    return pltpu.roll(v, 1, axis=0)


def y_next(v):
    return pltpu.roll(v, v.shape[1] - 1, axis=1)


def y_prev(v):
    return pltpu.roll(v, 1, axis=1)


def main_tile(v):
    return v[8:24, 0:128]


def well_grids(lists_main, lists_side, missing_n, missing_s, missing_e, missing_w):
    lane = lax.broadcasted_iota(jnp.int32, (1, 128), 1)
    low = lane < 64
    side = [jnp.where(low, e, w) for e, w in lists_side]

    def ids(cells, drop):
        cells = cells.astype(jnp.int32)
        row = lax.shift_right_logical(cells, 7)
        col = jnp.bitwise_and(cells, 127)
        return row - 1024 * drop, col

    def columns(col):
        at = lax.broadcasted_iota(jnp.int32, (128, 128), 0)
        return jnp.where(at == col, 1.0, 0.0).astype(jnp.bfloat16)

    def split(v):
        hi = v.astype(jnp.bfloat16).astype(jnp.float32)
        mid = (v - hi).astype(jnp.bfloat16).astype(jnp.float32)
        return hi, mid, v - hi - mid

    def product(row, col_hot, value_rows, first, extra):
        count = 32 + (8 if extra else 0)
        at = lax.broadcasted_iota(jnp.int32, (32, 128), 0)
        at = lax.shift_right_logical(at, 3) * 16 + jnp.bitwise_and(at, 7) + first
        hit = row == at
        lhs = []
        for blocks in value_rows:
            lhs.append(
                jnp.concatenate([jnp.where(hit, b, 0.0) for b in blocks], axis=1)
            )
        if extra:
            at = lax.broadcasted_iota(jnp.int32, (8, 128), 0) * 16 + 8
            hit = row == at
            lhs.append(jnp.concatenate([jnp.where(hit, b, 0.0) for b in value_rows[0]], axis=1))
        lhs = jnp.concatenate(lhs, axis=0).astype(jnp.bfloat16)
        rhs = jnp.concatenate([col_hot] * len(value_rows[0]), axis=1)
        return lax.dot_general(
            lhs, rhs, (((1,), (1,)), ((), ())), preferred_element_type=jnp.float32
        )

    zero = jnp.zeros((1, 128), jnp.float32)

    def main_values(tile):
        out = []
        for q in range(1, 7):
            hi, mid, lo = split(tile[q : q + 1])
            out.append([jnp.where(low, hi, mid), jnp.where(low, lo, zero)])
        out.append([jnp.where(low, zero + 1.0, zero), zero])
        return out

    def side_values(tile):
        out = []
        for q in range(1, 7):
            out.append(list(split(tile[q : q + 1])))
        out.append([zero + 1.0, zero, zero])
        return out

    def main_part(tile, drop):
        row, col = ids(tile[0:1], drop)
        return row, columns(col), main_values(tile)

    def side_part(tile, drop):
        row, col = ids(tile[0:1], drop + jnp.where(low, missing_e, missing_w))
        col = jnp.where(low, jnp.where(col < 64, col, -1), jnp.where(col < 64, -1, col))
        return row, columns(col), side_values(tile)

    n, c, s = [main_part(t, d) for t, d in zip(lists_main, (missing_n, 0, missing_s))]
    sn, sc, ss = [side_part(t, d) for t, d in zip(side, (missing_n, 0, missing_s))]
    mains = [
        product(*n, 8, False), product(*c, 0, False), product(*c, 8, False), product(*s, 0, True)
    ]
    sides = [
        product(*sn, 8, False), product(*sc, 0, False), product(*sc, 8, False),
        product(*ss, 0, False),
    ]
    grids = []
    for q in range(7):
        layers = []
        for layer in range(4):
            at = (q * 4 + layer) * 8
            layers.append(
                jnp.concatenate(
                    [
                        jnp.concatenate([m[at : at + 8], d[at : at + 8]], axis=1)
                        for m, d in zip(mains, sides)
                    ],
                    axis=0,
                )
            )
        grids.append(layers)
    return grids, mains[3][224:232]


def compute_kernel(
    own, own_list, from_n, from_s, ext_n, ext_s, from_e, from_w, from_ne, from_nw, from_se, from_sw,
    out_x, out_y, out_z,
):
    gx, gy = lax.axis_index("gx"), lax.axis_index("gy")
    nx, ny = lax.axis_size("gx"), lax.axis_size("gy")
    miss_n, miss_s = gx == 0, gx == nx - 1
    miss_w, miss_e = gy == 0, gy == ny - 1
    shape = (32, 256)
    row = lax.broadcasted_iota(jnp.int32, shape, 0)
    lane = lax.broadcasted_iota(jnp.int32, shape, 1)

    row_low = jnp.where(miss_n, 8, 0)
    row_high = jnp.where(miss_s, 24, 32)
    lane_low = jnp.where(miss_e, 192, 128)
    lane_high = jnp.where(miss_w, 192, 256)
    row_ok = (row >= row_low) & (row < row_high)
    lane_ok = (lane < 128) | ((lane >= lane_low) & (lane < lane_high))
    valid = row_ok & lane_ok
    keep_x = valid & jnp.logical_not((row == 23) & miss_s)
    keep_y = valid & jnp.logical_not((lane == 127) & miss_e)

    block = lax.broadcasted_iota(jnp.int32, (8, 128), 1) // 16
    even = jnp.bitwise_and(block, 1) == 0
    merged = []
    for e_ref, w_ref, base in (
        (from_ne, from_nw, 0), (from_e, from_w, 1), (from_e, from_w, 5), (from_se, from_sw, 2)
    ):
        pairs = []
        for group in range(GROUPS):
            e, w = e_ref[base + group], w_ref[base + group]
            pairs.append((jnp.where(even, e, w), jnp.where(even, w, e)))
        merged.append(pairs)

    def field(slot, mask, fill):
        group, k = slot // 8, slot % 8
        sides = []
        for j in range(4):
            tile = merged[j][group][k % 2]
            sides.append(pltpu.roll(tile, 128 - 16 * k, axis=1) if k else tile)
        mains = [from_n[slot], own[slot], from_s[slot]]
        whole = jnp.concatenate(
            [jnp.concatenate(mains, axis=0), jnp.concatenate(sides, axis=0)], axis=1
        )
        return jnp.where(mask, whole, fill)

    L = range(4)
    p0 = [field(P0 + l, valid, 0.0) for l in L]
    s0 = [field(S0 + l, valid, 0.0) for l in L]
    tx = [field(TX + l, keep_x, 0.0) for l in L]
    ty = [field(TY + l, keep_y, 0.0) for l in L]
    tz = [field(TZ + l, valid, 0.0) for l in range(3)]
    pv = [field(PV + l, valid, 1.0) for l in L]
    up = [field(UP + l, valid, 0.0).astype(jnp.int32) for l in L]

    (src0, src1, obs_p0, obs_s0, obs_p1, obs_s1, count), src0_extra = well_grids(
        (ext_n[1], own_list[...], ext_s[4]),
        ((from_ne[4], from_nw[4]), (from_e[0], from_w[0]), (from_se[1], from_sw[1])),
        *[jnp.where(miss, 1, 0) for miss in (miss_n, miss_s, miss_e, miss_w)],
    )
    src, obs_p, obs_s = (src0, src1), (obs_p0, obs_p1), (obs_s0, obs_s1)

    row8 = lax.broadcasted_iota(jnp.int32, (8, 256), 0)

    def first_row(v, extra):
        top = jnp.where(row8 == 0, jnp.concatenate([extra, extra], axis=1), v[0:8])
        return jnp.concatenate([top, v[8:32]], axis=0)

    def last_row(v, extra):
        tail = jnp.where(row8 == 7, jnp.concatenate([extra, extra], axis=1), v[24:32])
        return jnp.concatenate([v[0:24], tail], axis=0)

    edge_n = jnp.where(miss_n, 0.0, ext_n[0])
    txw = [first_row(x_prev(tx[l]), edge_n[4 + l : 5 + l]) for l in L]
    tyw = [y_prev(ty[l]) for l in L]

    def z_sum(faces, values, l):
        total = None
        if l < 3:
            total = faces[l] * values[l + 1]
        if l > 0:
            term = faces[l - 1] * values[l - 1]
            total = term if total is None else total + term
        return total

    ones = [None] * 4
    inv = []
    for l in L:
        den = pv[l] + tx[l] + txw[l] + ty[l] + tyw[l]
        if l < 3:
            den = den + tz[l]
        if l > 0:
            den = den + tz[l - 1]
        inv.append(1.0 / den)

    def gather(values, nexts, prevs):
        out = []
        for l in L:
            total = tx[l] * nexts[l] + txw[l] * prevs[l]
            total = total + ty[l] * y_next(values[l]) + tyw[l] * y_prev(values[l])
            out.append(total + z_sum(tz, values, l))
        return out

    sub8 = lax.broadcasted_iota(jnp.int32, (8, 128), 0)
    cut = lambda t: jnp.where(miss_s, 0.0, t)
    t0 = ext_s[0]
    lane8 = lax.broadcasted_iota(jnp.int32, (8, 128), 1)
    side0 = jnp.where(lane8 < 64, jnp.where(miss_e, 0.0, from_se[0]), jnp.where(miss_w, 0.0, from_sw[0]))
    t0 = jnp.concatenate([cut(t0), cut(side0)], axis=1)
    t0n, t0p = y_next(t0)[:, 0:128], y_prev(t0)[:, 0:128]
    t0 = t0[:, 0:128]
    t1, t2, t3 = cut(ext_s[1]), cut(ext_s[2]), cut(ext_s[3])
    low4 = lambda t: pltpu.roll(t, 4, axis=0)
    ty_x = jnp.where((lane8 == 127) & miss_e, 0.0, low4(t0))
    tyw_x = low4(t0p)
    tx_x, txw_x = low4(t2), t2
    pv_x = jnp.where(miss_s, 1.0, t3)
    tz_x = jnp.where(sub8 < 3, low4(t3), 0.0)
    tzw_x = jnp.where((sub8 >= 1) & (sub8 < 4), pltpu.roll(low4(t3), 1, axis=0), 0.0)
    num_x = (
        pv_x * t0 + src0_extra + tx_x * low4(t1) + txw_x * t1 + ty_x * t0n + tyw_x * t0p
        + tz_x * pltpu.roll(t0, 7, axis=0) + tzw_x * pltpu.roll(t0, 1, axis=0)
    )
    q_extra = num_x / (pv_x + tx_x + txw_x + ty_x + tyw_x + tz_x + tzw_x)

    bits = [[[jnp.bitwise_and(up[l], 1 << (3 * n + d)) != 0 for d in range(3)] for l in L] for n in range(2)]

    ipv = [time_step / pv[l] for l in L]
    saved = []
    p, s = p0, s0
    for n in range(2):
        p_next = [x_next(p[l]) for l in L]
        p_prev = [x_prev(p[l]) for l in L]
        if n == 0:
            p_prev = [first_row(p_prev[l], edge_n[l : l + 1]) for l in L]
        base = [pv[l] * p[l] + src[n][l] for l in L]
        total = gather(p, p_next, p_prev)
        q = [(base[l] + total[l]) * inv[l] for l in L]
        q_next = [x_next(q[l]) for l in L]
        if n == 0:
            q_next = [last_row(q_next[l], q_extra[l : l + 1]) for l in L]
        total = gather(q, q_next, [x_prev(q[l]) for l in L])
        r = [(base[l] + total[l]) * inv[l] for l in L]

        den = []
        mob = []
        for l in L:
            wet = s[l] * s[l]
            dry = 1.0 - s[l]
            scale = 1.0 / (wet + 0.5 * dry * dry)
            den.append(scale)
            mob.append(wet * scale)
        dx = [r[l] - x_next(r[l]) for l in L]
        dy = [r[l] - y_next(r[l]) for l in L]
        dz = [r[l] - r[l + 1] for l in range(3)]
        fx = [jnp.where(bits[n][l][0], mob[l], x_next(mob[l])) for l in L]
        fy = [jnp.where(bits[n][l][1], mob[l], y_next(mob[l])) for l in L]
        fz = [jnp.where(bits[n][l][2], mob[l], mob[l + 1]) for l in range(3)]
        flow_x = [tx[l] * dx[l] * fx[l] for l in L]
        flow_y = [ty[l] * dy[l] * fy[l] for l in L]
        flow_z = [tz[l] * dz[l] * fz[l] for l in range(3)]
        moved = []
        for l in L:
            net = flow_x[l] - x_prev(flow_x[l]) + flow_y[l] - y_prev(flow_y[l])
            if l < 3:
                net = net + flow_z[l]
            if l > 0:
                net = net - flow_z[l - 1]
            moved.append(s[l] - ipv[l] * net)
        saved.append((p, q, r, s, den, dx, dy, dz, fx, fy, fz))
        p, s = r, moved

    grad_x = [None] * 4
    grad_y = [None] * 4
    grad_z = [None] * 3

    def accumulate(total, term):
        return term if total is None else total + term

    carried_p = [count[l] * p[l] - obs_p[1][l] for l in L]
    carried_s = [count[l] * s[l] - obs_s[1][l] for l in L]
    for n in (1, 0):
        p, q, r, s, den, dx, dy, dz, fx, fy, fz = saved[n]
        nu = [ipv[l] * carried_s[l] for l in L]
        mx = [x_next(nu[l]) - nu[l] for l in L]
        my = [y_next(nu[l]) - nu[l] for l in L]
        mz = [nu[l + 1] - nu[l] for l in range(3)]
        for l in L:
            grad_x[l] = accumulate(
                grad_x[l], main_tile(mx[l]) * main_tile(dx[l]) * main_tile(fx[l])
            )
            grad_y[l] = accumulate(
                grad_y[l], main_tile(my[l]) * main_tile(dy[l]) * main_tile(fy[l])
            )
            if l < 3:
                grad_z[l] = accumulate(
                    grad_z[l], main_tile(mz[l]) * main_tile(dz[l]) * main_tile(fz[l])
                )
        gx_ = [mx[l] * tx[l] for l in L]
        gy_ = [my[l] * ty[l] for l in L]
        gz_ = [mz[l] * tz[l] for l in range(3)]
        hx = [gx_[l] * fx[l] for l in L]
        hy = [gy_[l] * fy[l] for l in L]
        hz = [gz_[l] * fz[l] for l in range(3)]
        pi = []
        for l in L:
            total = carried_p[l] + hx[l] - x_prev(hx[l]) + hy[l] - y_prev(hy[l])
            if l < 3:
                total = total + hz[l]
            if l > 0:
                total = total - hz[l - 1]
            pi.append(total)
        if n:
            kx = [gx_[l] * dx[l] for l in L]
            ky = [gy_[l] * dy[l] for l in L]
            kz = [gz_[l] * dz[l] for l in range(3)]
            back_s = []
            for l in L:
                here = jnp.where(bits[n][l][0], kx[l], 0.0)
                there = kx[l] - here
                total = here + x_prev(there)
                here = jnp.where(bits[n][l][1], ky[l], 0.0)
                there = ky[l] - here
                total = total + here + y_prev(there)
                if l < 3:
                    total = total + jnp.where(bits[n][l][2], kz[l], 0.0)
                if l > 0:
                    total = total + jnp.where(bits[n][l - 1][2], 0.0, kz[l - 1])
                slope = (s[l] * den[l]) * ((1.0 - s[l]) * den[l])
                back_s.append(
                    carried_s[l] + slope * total + (count[l] * s[l] - obs_s[0][l])
                )
            carried_s = back_s

        w2 = [pi[l] * inv[l] for l in L]
        w2_next = [x_next(w2[l]) for l in L]
        rho = gather(w2, w2_next, [x_prev(w2[l]) for l in L])
        w1 = [rho[l] * inv[l] for l in L]
        w1_next = [x_next(w1[l]) for l in L]
        m = main_tile
        for l in L:
            a2, a1 = m(w2[l]), m(w1[l])
            rm, qm, pm = m(r[l]), m(q[l]), m(p[l])
            grad_x[l] = (
                grad_x[l]
                + a2 * (m(x_next(q[l])) - rm)
                + m(w2_next[l]) * (qm - m(x_next(r[l])))
                + a1 * (m(x_next(p[l])) - qm)
                + m(w1_next[l]) * (pm - m(x_next(q[l])))
            )
            grad_y[l] = (
                grad_y[l]
                + a2 * (m(y_next(q[l])) - rm)
                + m(y_next(w2[l])) * (qm - m(y_next(r[l])))
                + a1 * (m(y_next(p[l])) - qm)
                + m(y_next(w1[l])) * (pm - m(y_next(q[l])))
            )
            if l < 3:
                grad_z[l] = (
                    grad_z[l]
                    + a2 * (m(q[l + 1]) - rm)
                    + m(w2[l + 1]) * (qm - m(r[l + 1]))
                    + a1 * (m(p[l + 1]) - qm)
                    + m(w1[l + 1]) * (pm - m(q[l + 1]))
                )
        if n:
            back = gather(w1, w1_next, [x_prev(w1[l]) for l in L])
            carried_p = [
                back[l] + pv[l] * (w1[l] + w2[l]) + (count[l] * p[l] - obs_p[0][l]) for l in L
            ]

    for l in L:
        out_x[l] = jnp.where(main_tile(keep_x), grad_x[l], 0.0)
        out_y[l] = jnp.where(main_tile(keep_y), grad_y[l], 0.0)
        if l < 3:
            out_z[l] = grad_z[l]


def compute(*args):
    f32 = jnp.float32
    return pl.pallas_call(
        compute_kernel,
        out_shape=(
            jax.ShapeDtypeStruct((4, 16, 128), f32),
            jax.ShapeDtypeStruct((4, 16, 128), f32),
            jax.ShapeDtypeStruct((3, 16, 128), f32),
        ),
        in_specs=[pl.BlockSpec(memory_space=pltpu.VMEM)] * 12,
        out_specs=[pl.BlockSpec(memory_space=pltpu.VMEM)] * 3,
    )(*args)


def on_device(*args):
    return compute(*exchange(*args))


def solution(mesh):
    field = P(None, "gx", "gy")
    in_specs = (field,) * 7 + (
        P("gx", "gy", None),
        P("gx", "gy", None),
        P(None, "gx", "gy", None),
        P(None, None, "gx", "gy", None),
    )
    return jax.shard_map(
        on_device, mesh=mesh, in_specs=in_specs, out_specs=(field,) * 3, check_vma=False
    )
```

time: 362 us -> 29.8 us (0.08)
  the two profiles are of different devices: /device:TPU:56 before, /device:TPU:1 now
where the time goes in v1:
time: 29.8 us; the launch traced here: 29.6 us
  Pallas kernels  28.9 us (97%)
  between operations  0.64 us (2%)
    pallas_call x1, Pallas kernels, exchange(): pl.pallas_call(exchange_kernel, out_shape=outs, in_specs=[pl.BlockSpec(me...  25.3 us
    pallas_call x1, Pallas kernels, compute(): pl.pallas_call(compute_kernel, out_shape=(jax.ShapeDtypeStruct((4, 16, 12...  3.62 us

profile of v1, /device:TPU:1, one launch (start us, length us, event | category | flops | bytes accessed | tf_op | source)
XLA Modules:
  0.0 29.6 jit_solution(13310003747759623037)
XLA Ops:
  0.6 25.3 %shard_map.130 = (f32[27,16,128]{2,1,0:T(8,128)}, f32[8,128]{1,0:T(8,128)}, f32[27,8,128]{2,1,0:T(8,128)}, f32[27,8,128]{2,1,0:T(8,128)}, f32[2,8,128]{2,1,0:T(8...) custom-call(f32[4,16,128]{2,1,0:T(8,128)} %p0.1, ...), custom_call_target="tpu_custom_call" | custom-call | tf_op jit(solution)/shard_map/pallas_call | solution.py:139
  26.0 3.6 %shard_map.131 = (f32[4,16,128]{2,1,0:T(8,128)}, f32[4,16,128]{2,1,0:T(8,128)}, f32[3,16,128]{2,1,0:T(8,128)}) custom-call(f32[27,16,128]{2,1,0:T(8,128)} %get-tuple-element.15.own, f32[8,128]{1,0:T(8,128)} %get-tuple-element.16.own_list, f32[27,8,128]{2,1,0:T(8,128)} %get-tuple-element.17.from_n, f32[27,8,128]{2,1,0:T(8,128)} %get-tuple-element.18.from_s, ...), custom_call_target="tpu_custom_call" | custom-call | tf_op jit(solution)/shard_map/pallas_call | solution.py:555

commit v2 on v1

--- a/solution.py
+++ b/solution.py
@@ -15,41 +15,67 @@
 
 def exchange_kernel(
     p0, s0, tx, ty, tz, pv, up, cell, rate, plan, observed,
-    own, own_list, from_n, from_s, ext_n, ext_s, from_e, from_w, from_ne, from_nw, from_se, from_sw,
-    up_int, cell_v, rate_v, plan_v, obs_v, xtra_n, xtra_s, pack_e, pack_w, in_sem, send_sem, recv_sem,
+    own, own_up, own_list, from_n, from_s, up_n, up_s, ext_n, ext_s,
+    from_e, from_w, from_ne, from_nw, from_se, from_sw,
+    cell_v, rate_v, plan_v, obs_v, xtra_n, xtra_s, pack_e, pack_w, in_sem, send_sem, recv_sem,
 ):
     gx, gy = lax.axis_index("gx"), lax.axis_index("gy")
     nx, ny = lax.axis_size("gx"), lax.axis_size("gy")
-    north, south = lax.rem(gx + nx - 1, nx), lax.rem(gx + 1, nx)
-    west, east = lax.rem(gy + ny - 1, ny), lax.rem(gy + 1, ny)
+    has_n, has_s = gx > 0, gx < nx - 1
+    has_w, has_e = gy > 0, gy < ny - 1
+    both = jnp.logical_and
+    peers = (
+        (has_n, (gx - 1, gy)),
+        (has_s, (gx + 1, gy)),
+        (has_e, (gx, gy + 1)),
+        (has_w, (gx, gy - 1)),
+        (both(has_n, has_e), (gx - 1, gy + 1)),
+        (both(has_n, has_w), (gx - 1, gy - 1)),
+        (both(has_s, has_e), (gx + 1, gy + 1)),
+        (both(has_s, has_w), (gx + 1, gy - 1)),
+    )
+    N, S, E, W, NE, NW, SE, SW = range(8)
 
     barrier = pltpu.get_barrier_semaphore()
-    for peer in (
-        (north, gy), (south, gy), (gx, east), (gx, west),
-        (south, east), (south, west), (north, east), (north, west),
-    ):
-        pl.semaphore_signal(barrier, inc=1, device_id=peer, device_id_type=MESH)
-
-    loads = [
-        (p0, own.at[pl.ds(P0, 4)]),
-        (s0, own.at[pl.ds(S0, 4)]),
-        (tx, own.at[pl.ds(TX, 4)]),
-        (ty, own.at[pl.ds(TY, 4)]),
-        (tz, own.at[pl.ds(TZ, 3)]),
-        (pv, own.at[pl.ds(PV, 4)]),
-        (up, up_int),
-        (cell, cell_v),
-        (rate, rate_v),
-        (plan, plan_v),
-        (observed, obs_v),
-    ]
+    for here, peer in peers:
+        @pl.when(here)
+        def _():
+            pl.semaphore_signal(barrier, inc=1, device_id=peer, device_id_type=MESH)
+
+    fields = ((p0, P0, 4), (tx, TX, 4), (ty, TY, 4), (tz, TZ, 3), (pv, PV, 4), (s0, S0, 4))
+    loads = [(ref, own.at[pl.ds(slot, n)]) for ref, slot, n in fields]
+    loads += [(up, own_up), (cell, cell_v), (rate, rate_v), (plan, plan_v), (observed, obs_v)]
     loads = [pltpu.make_async_copy(a, b, in_sem.at[i]) for i, (a, b) in enumerate(loads)]
     for load in loads:
         load.start()
+
+    rows = jnp.where(has_n, 1, 0) + jnp.where(has_s, 1, 0) + 1
+    columns = jnp.where(has_e, 1, 0) + jnp.where(has_w, 1, 0) + 1
+    pl.semaphore_wait(barrier, rows * columns - 1)
+
+    sends = []
+
+    def send(src, dst, to, origin):
+        at = len(sends)
+        here, peer = peers[to]
+        copy = pltpu.make_async_remote_copy(
+            src_ref=src, dst_ref=dst, send_sem=send_sem.at[at], recv_sem=recv_sem.at[at],
+            device_id=peer, device_id_type=MESH,
+        )
+        sends.append((copy, here, peers[origin][0]))
+
+        @pl.when(here)
+        def _():
+            copy.start()
+
+    for ref, slot, n in fields:
+        send(ref.at[:, pl.ds(0, 8), :], from_s.at[pl.ds(slot, n)], N, S)
+        send(ref.at[:, pl.ds(8, 8), :], from_n.at[pl.ds(slot, n)], S, N)
+    send(up.at[:, pl.ds(0, 8), :], up_s, N, S)
+    send(up.at[:, pl.ds(8, 8), :], up_n, S, N)
+
     for load in loads:
         load.wait()
-
-    own[UP:SLOTS] = up_int[...].astype(jnp.float32)
 
     rates = rate_v[0] * 0.5
     rows = [
@@ -81,6 +107,8 @@
     xtra_s[3, 7:8] = jnp.zeros((1, 128), jnp.float32)
     xtra_s[4] = wells
     xtra_n[1] = wells
+    send(xtra_s, ext_s, N, S)
+    send(xtra_n, ext_n, S, N)
 
     block = lax.broadcasted_iota(jnp.int32, (8, 128), 1) // 16
     for pack in (pack_e, pack_w):
@@ -91,7 +119,11 @@
         for group in range(GROUPS):
             first = second = None
             for k in range(min(8, SLOTS - 8 * group)):
-                tile = own[8 * group + k, 8 * half : 8 * half + 8]
+                slot = 8 * group + k
+                if slot < UP:
+                    tile = own[slot, 8 * half : 8 * half + 8]
+                else:
+                    tile = own_up[slot - UP, 8 * half : 8 * half + 8].astype(jnp.float32)
                 if k:
                     tile = pltpu.roll(tile, 16 * k, axis=1)
                 first = tile if first is None else jnp.where(block == k, tile, first)
@@ -99,40 +131,31 @@
             pack_e[2 + 4 * half + group] = first
             pack_w[2 + 4 * half + group] = second
 
-    pl.semaphore_wait(barrier, 8)
-
-    sends = [
-        (own.at[:, pl.ds(0, 8), :], from_s, (north, gy)),
-        (own.at[:, pl.ds(8, 8), :], from_n, (south, gy)),
-        (xtra_s, ext_s, (north, gy)),
-        (xtra_n, ext_n, (south, gy)),
-        (pack_w.at[pl.ds(1, 9)], from_w, (gx, east)),
-        (pack_e.at[pl.ds(1, 9)], from_e, (gx, west)),
-        (pack_w.at[pl.ds(6, 5)], from_nw, (south, east)),
-        (pack_e.at[pl.ds(6, 5)], from_ne, (south, west)),
-        (pack_w.at[pl.ds(0, 6)], from_sw, (north, east)),
-        (pack_e.at[pl.ds(0, 6)], from_se, (north, west)),
-    ]
-    sends = [
-        pltpu.make_async_remote_copy(
-            src_ref=src, dst_ref=dst, send_sem=send_sem.at[i], recv_sem=recv_sem.at[i],
-            device_id=peer, device_id_type=MESH,
-        )
-        for i, (src, dst, peer) in enumerate(sends)
-    ]
-    for send in sends:
-        send.start()
-    for send in sends:
-        send.wait()
+    send(pack_w.at[pl.ds(1, 9)], from_w, E, W)
+    send(pack_e.at[pl.ds(1, 9)], from_e, W, E)
+    send(pack_w.at[pl.ds(6, 5)], from_nw, SE, NW)
+    send(pack_e.at[pl.ds(6, 5)], from_ne, SW, NE)
+    send(pack_w.at[pl.ds(0, 6)], from_sw, NE, SW)
+    send(pack_e.at[pl.ds(0, 6)], from_se, NW, SE)
+    for copy, here, origin in sends:
+        @pl.when(origin)
+        def _():
+            copy.wait_recv()
+    for copy, here, origin in sends:
+        @pl.when(here)
+        def _():
+            copy.wait_send()
 
 
 def exchange(*args):
     f32 = jnp.float32
     tile = lambda *lead: jax.ShapeDtypeStruct(lead + (8, 128), f32)
+    ints = lambda *shape: jax.ShapeDtypeStruct(shape, jnp.int32)
     outs = (
-        jax.ShapeDtypeStruct((SLOTS, 16, 128), f32),
+        jax.ShapeDtypeStruct((UP, 16, 128), f32),
+        ints(4, 16, 128),
         tile(),
-        tile(SLOTS), tile(SLOTS), tile(2), tile(5),
+        tile(UP), tile(UP), ints(4, 8, 128), ints(4, 8, 128), tile(2), tile(5),
         tile(9), tile(9),
         tile(5), tile(5), tile(6), tile(6),
     )
@@ -140,9 +163,8 @@
         exchange_kernel,
         out_shape=outs,
         in_specs=[pl.BlockSpec(memory_space=pl.ANY)] * 11,
-        out_specs=[pl.BlockSpec(memory_space=pltpu.VMEM)] * 12,
+        out_specs=[pl.BlockSpec(memory_space=pltpu.VMEM)] * len(outs),
         scratch_shapes=[
-            pltpu.VMEM((4, 16, 128), jnp.int32),
             pltpu.VMEM((1, 1, WELLS), jnp.int32),
             pltpu.VMEM((1, 1, WELLS), f32),
             pltpu.VMEM((2, 1, 1, WELLS), jnp.int32),
@@ -152,8 +174,8 @@
             pltpu.VMEM((11, 8, 128), f32),
             pltpu.VMEM((11, 8, 128), f32),
             pltpu.SemaphoreType.DMA((11,)),
-            pltpu.SemaphoreType.DMA((10,)),
-            pltpu.SemaphoreType.DMA((10,)),
+            pltpu.SemaphoreType.DMA((22,)),
+            pltpu.SemaphoreType.DMA((22,)),
         ],
         compiler_params=pltpu.CompilerParams(collective_id=0, has_side_effects=True),
     )(*args)
@@ -273,7 +295,8 @@
 
 
 def compute_kernel(
-    own, own_list, from_n, from_s, ext_n, ext_s, from_e, from_w, from_ne, from_nw, from_se, from_sw,
+    own, own_up, own_list, from_n, from_s, up_n, up_s, ext_n, ext_s,
+    from_e, from_w, from_ne, from_nw, from_se, from_sw,
     out_x, out_y, out_z,
 ):
     gx, gy = lax.axis_index("gx"), lax.axis_index("gy")
@@ -312,7 +335,11 @@
         for j in range(4):
             tile = merged[j][group][k % 2]
             sides.append(pltpu.roll(tile, 128 - 16 * k, axis=1) if k else tile)
-        mains = [from_n[slot], own[slot], from_s[slot]]
+        if slot < UP:
+            mains = [from_n[slot], own[slot], from_s[slot]]
+        else:
+            mains = [up_n[slot - UP], own_up[slot - UP], up_s[slot - UP]]
+            sides = [side.astype(jnp.int32) for side in sides]
         whole = jnp.concatenate(
             [jnp.concatenate(mains, axis=0), jnp.concatenate(sides, axis=0)], axis=1
         )
@@ -325,7 +352,7 @@
     ty = [field(TY + l, keep_y, 0.0) for l in L]
     tz = [field(TZ + l, valid, 0.0) for l in range(3)]
     pv = [field(PV + l, valid, 1.0) for l in L]
-    up = [field(UP + l, valid, 0.0).astype(jnp.int32) for l in L]
+    up = [field(UP + l, valid, 0) for l in L]
 
     (src0, src1, obs_p0, obs_s0, obs_p1, obs_s1, count), src0_extra = well_grids(
         (ext_n[1], own_list[...], ext_s[4]),
@@ -559,7 +586,7 @@
             jax.ShapeDtypeStruct((4, 16, 128), f32),
             jax.ShapeDtypeStruct((3, 16, 128), f32),
         ),
-        in_specs=[pl.BlockSpec(memory_space=pltpu.VMEM)] * 12,
+        in_specs=[pl.BlockSpec(memory_space=pltpu.VMEM)] * 15,
         out_specs=[pl.BlockSpec(memory_space=pltpu.VMEM)] * 3,
     )(*args)
 

time: 29.8 us -> 25.6 us (0.86)
  the two profiles are of different devices: /device:TPU:1 before, /device:TPU:56 now
where the time goes in v2:
time: 25.6 us; the launch traced here: 25.1 us
  Pallas kernels  24.4 us (95%)
  between operations  0.64 us (2%)
    pallas_call x1, Pallas kernels, exchange(): pl.pallas_call(exchange_kernel, out_shape=outs, in_specs=[pl.BlockSpec(me...  20.8 us
    pallas_call x1, Pallas kernels, compute(): pl.pallas_call(compute_kernel, out_shape=(jax.ShapeDtypeStruct((4, 16, 12...  3.64 us

profile of v2, /device:TPU:56, one launch (start us, length us, event | category | flops | bytes accessed | tf_op | source)
XLA Modules:
  0.0 25.1 jit_solution(4235740358253643282)
XLA Ops:
  0.6 20.8 %shard_map.130 = (f32[23,16,128]{2,1,0:T(8,128)}, s32[4,16,128]{2,1,0:T(8,128)}, f32[8,128]{1,0:T(8,128)}, f32[23,8,128]{2,1,0:T(8,128)}, f32[23,8,128]{2,1,0:T(...) custom-call(f32[4,16,128]{2,1,0:T(8,128)} %p0.1, ...), custom_call_target="tpu_custom_call" | custom-call | tf_op jit(solution)/shard_map/pallas_call | solution.py:162
  21.4 3.6 %shard_map.131 = (f32[4,16,128]{2,1,0:T(8,128)}, f32[4,16,128]{2,1,0:T(8,128)}, f32[3,16,128]{2,1,0:T(8,128)}) custom-call(f32[23,16,128]{2,1,0:T(8,128)} %get-tuple-element.18.own, s32[4,16,128]{2,1,0:T(8,128)} %get-tuple-element.19.own_up, f32[8,128]{1,0:T(8,128)} %get-tuple-element.20.own_list, f32[23,8,128]{2,1,0:T(8,128)} %get-tuple-element.21.from_n, ...), custom_call_target="tpu_custom_call" | custom-call | tf_op jit(solution)/shard_map/pallas_call | solution.py:582

commit v3 on v2

--- a/solution.py
+++ b/solution.py
@@ -13,12 +13,12 @@
 WELLS = 64
 
 
-def exchange_kernel(
-    p0, s0, tx, ty, tz, pv, up, cell, rate, plan, observed,
-    own, own_up, own_list, from_n, from_s, up_n, up_s, ext_n, ext_s,
-    from_e, from_w, from_ne, from_nw, from_se, from_sw,
-    cell_v, rate_v, plan_v, obs_v, xtra_n, xtra_s, pack_e, pack_w, in_sem, send_sem, recv_sem,
-):
+def start_exchange(args, halo, work, sems):
+    p0, s0, tx, ty, tz, pv, up, cell, rate, plan, observed = args
+    own, own_up, own_list, from_n, from_s, up_n, up_s, ext_n, ext_s = halo[:9]
+    from_e, from_w, from_ne, from_nw, from_se, from_sw = halo[9:]
+    cell_v, rate_v, plan_v, obs_v, xtra_n, xtra_s, pack_e, pack_w = work
+    in_sem, send_sem, recv_sem = sems
     gx, gy = lax.axis_index("gx"), lax.axis_index("gy")
     nx, ny = lax.axis_size("gx"), lax.axis_size("gy")
     has_n, has_s = gx > 0, gx < nx - 1
@@ -49,31 +49,6 @@
     for load in loads:
         load.start()
 
-    rows = jnp.where(has_n, 1, 0) + jnp.where(has_s, 1, 0) + 1
-    columns = jnp.where(has_e, 1, 0) + jnp.where(has_w, 1, 0) + 1
-    pl.semaphore_wait(barrier, rows * columns - 1)
-
-    sends = []
-
-    def send(src, dst, to, origin):
-        at = len(sends)
-        here, peer = peers[to]
-        copy = pltpu.make_async_remote_copy(
-            src_ref=src, dst_ref=dst, send_sem=send_sem.at[at], recv_sem=recv_sem.at[at],
-            device_id=peer, device_id_type=MESH,
-        )
-        sends.append((copy, here, peers[origin][0]))
-
-        @pl.when(here)
-        def _():
-            copy.start()
-
-    for ref, slot, n in fields:
-        send(ref.at[:, pl.ds(0, 8), :], from_s.at[pl.ds(slot, n)], N, S)
-        send(ref.at[:, pl.ds(8, 8), :], from_n.at[pl.ds(slot, n)], S, N)
-    send(up.at[:, pl.ds(0, 8), :], up_s, N, S)
-    send(up.at[:, pl.ds(8, 8), :], up_n, S, N)
-
     for load in loads:
         load.wait()
 
@@ -107,8 +82,6 @@
     xtra_s[3, 7:8] = jnp.zeros((1, 128), jnp.float32)
     xtra_s[4] = wells
     xtra_n[1] = wells
-    send(xtra_s, ext_s, N, S)
-    send(xtra_n, ext_n, S, N)
 
     block = lax.broadcasted_iota(jnp.int32, (8, 128), 1) // 16
     for pack in (pack_e, pack_w):
@@ -131,54 +104,38 @@
             pack_e[2 + 4 * half + group] = first
             pack_w[2 + 4 * half + group] = second
 
-    send(pack_w.at[pl.ds(1, 9)], from_w, E, W)
-    send(pack_e.at[pl.ds(1, 9)], from_e, W, E)
+    rows = jnp.where(has_n, 1, 0) + jnp.where(has_s, 1, 0) + 1
+    columns = jnp.where(has_e, 1, 0) + jnp.where(has_w, 1, 0) + 1
+    pl.semaphore_wait(barrier, rows * columns - 1)
+
+    sends = []
+
+    def send(src, dst, to, origin):
+        at = len(sends)
+        here, peer = peers[to]
+        copy = pltpu.make_async_remote_copy(
+            src_ref=src, dst_ref=dst, send_sem=send_sem.at[at], recv_sem=recv_sem.at[at],
+            device_id=peer, device_id_type=MESH,
+        )
+        sends.append((copy, here, peers[origin][0]))
+
+        @pl.when(here)
+        def _():
+            copy.start()
+
     send(pack_w.at[pl.ds(6, 5)], from_nw, SE, NW)
     send(pack_e.at[pl.ds(6, 5)], from_ne, SW, NE)
     send(pack_w.at[pl.ds(0, 6)], from_sw, NE, SW)
     send(pack_e.at[pl.ds(0, 6)], from_se, NW, SE)
-    for copy, here, origin in sends:
-        @pl.when(origin)
-        def _():
-            copy.wait_recv()
-    for copy, here, origin in sends:
-        @pl.when(here)
-        def _():
-            copy.wait_send()
-
-
-def exchange(*args):
-    f32 = jnp.float32
-    tile = lambda *lead: jax.ShapeDtypeStruct(lead + (8, 128), f32)
-    ints = lambda *shape: jax.ShapeDtypeStruct(shape, jnp.int32)
-    outs = (
-        jax.ShapeDtypeStruct((UP, 16, 128), f32),
-        ints(4, 16, 128),
-        tile(),
-        tile(UP), tile(UP), ints(4, 8, 128), ints(4, 8, 128), tile(2), tile(5),
-        tile(9), tile(9),
-        tile(5), tile(5), tile(6), tile(6),
-    )
-    return pl.pallas_call(
-        exchange_kernel,
-        out_shape=outs,
-        in_specs=[pl.BlockSpec(memory_space=pl.ANY)] * 11,
-        out_specs=[pl.BlockSpec(memory_space=pltpu.VMEM)] * len(outs),
-        scratch_shapes=[
-            pltpu.VMEM((1, 1, WELLS), jnp.int32),
-            pltpu.VMEM((1, 1, WELLS), f32),
-            pltpu.VMEM((2, 1, 1, WELLS), jnp.int32),
-            pltpu.VMEM((2, 2, 1, 1, WELLS), f32),
-            pltpu.VMEM((2, 8, 128), f32),
-            pltpu.VMEM((5, 8, 128), f32),
-            pltpu.VMEM((11, 8, 128), f32),
-            pltpu.VMEM((11, 8, 128), f32),
-            pltpu.SemaphoreType.DMA((11,)),
-            pltpu.SemaphoreType.DMA((22,)),
-            pltpu.SemaphoreType.DMA((22,)),
-        ],
-        compiler_params=pltpu.CompilerParams(collective_id=0, has_side_effects=True),
-    )(*args)
+    send(xtra_s, ext_s, N, S)
+    send(xtra_n, ext_n, S, N)
+    send(own.at[:, pl.ds(0, 8), :], from_s, N, S)
+    send(own.at[:, pl.ds(8, 8), :], from_n, S, N)
+    send(own_up.at[:, pl.ds(0, 8), :], up_s, N, S)
+    send(own_up.at[:, pl.ds(8, 8), :], up_n, S, N)
+    send(pack_w.at[pl.ds(1, 9)], from_w, E, W)
+    send(pack_e.at[pl.ds(1, 9)], from_e, W, E)
+    return sends
 
 
 def x_next(v):
@@ -294,11 +251,17 @@
     return grids, mains[3][224:232]
 
 
-def compute_kernel(
-    own, own_up, own_list, from_n, from_s, up_n, up_s, ext_n, ext_s,
-    from_e, from_w, from_ne, from_nw, from_se, from_sw,
-    out_x, out_y, out_z,
-):
+def adjoint_kernel(*refs):
+    args, out = refs[:11], refs[11]
+    halo, work, sems = refs[12:27], refs[27:35], refs[35:]
+    sends = start_exchange(args, halo, work, sems)
+    own, own_up, own_list, from_n, from_s, up_n, up_s, ext_n, ext_s = halo[:9]
+    from_e, from_w, from_ne, from_nw, from_se, from_sw = halo[9:]
+    for copy, here, origin in sends:
+        @pl.when(origin)
+        def _():
+            copy.wait_recv()
+
     gx, gy = lax.axis_index("gx"), lax.axis_index("gy")
     nx, ny = lax.axis_size("gx"), lax.axis_size("gy")
     miss_n, miss_s = gx == 0, gx == nx - 1
@@ -571,28 +534,69 @@
             ]
 
     for l in L:
-        out_x[l] = jnp.where(main_tile(keep_x), grad_x[l], 0.0)
-        out_y[l] = jnp.where(main_tile(keep_y), grad_y[l], 0.0)
+        out[l] = jnp.where(main_tile(keep_x), grad_x[l], 0.0)
+        out[4 + l] = jnp.where(main_tile(keep_y), grad_y[l], 0.0)
         if l < 3:
-            out_z[l] = grad_z[l]
-
-
-def compute(*args):
-    f32 = jnp.float32
+            out[8 + l] = grad_z[l]
+
+    for copy, here, origin in sends:
+        @pl.when(here)
+        def _():
+            copy.wait_send()
+
+
+def adjoint(*args):
+    f32, i32 = jnp.float32, jnp.int32
+    tiles = lambda n: pltpu.VMEM((n, 8, 128), f32)
+    halo = [
+        pltpu.VMEM((UP, 16, 128), f32),
+        pltpu.VMEM((4, 16, 128), i32),
+        pltpu.VMEM((8, 128), f32),
+        tiles(UP), tiles(UP),
+        pltpu.VMEM((4, 8, 128), i32), pltpu.VMEM((4, 8, 128), i32),
+        tiles(2), tiles(5), tiles(9), tiles(9), tiles(5), tiles(5), tiles(6), tiles(6),
+    ]
+    work = [
+        pltpu.VMEM((1, 1, WELLS), i32),
+        pltpu.VMEM((1, 1, WELLS), f32),
+        pltpu.VMEM((2, 1, 1, WELLS), i32),
+        pltpu.VMEM((2, 2, 1, 1, WELLS), f32),
+        tiles(2), tiles(5), tiles(11), tiles(11),
+    ]
+    sems = [pltpu.SemaphoreType.DMA((n,)) for n in (11, 12, 12)]
     return pl.pallas_call(
-        compute_kernel,
-        out_shape=(
-            jax.ShapeDtypeStruct((4, 16, 128), f32),
-            jax.ShapeDtypeStruct((4, 16, 128), f32),
-            jax.ShapeDtypeStruct((3, 16, 128), f32),
-        ),
-        in_specs=[pl.BlockSpec(memory_space=pltpu.VMEM)] * 15,
-        out_specs=[pl.BlockSpec(memory_space=pltpu.VMEM)] * 3,
+        adjoint_kernel,
+        out_shape=jax.ShapeDtypeStruct((11, 16, 128), f32),
+        in_specs=[pl.BlockSpec(memory_space=pl.ANY)] * 11,
+        out_specs=pl.BlockSpec(memory_space=pltpu.VMEM),
+        scratch_shapes=halo + work + sems,
+        compiler_params=pltpu.CompilerParams(collective_id=0, has_side_effects=True),
     )(*args)
 
 
+def deliver_kernel(stack, out_x, out_y, out_z, sem):
+    copies = [
+        pltpu.make_async_copy(stack.at[pl.ds(first, n)], out, sem.at[i])
+        for i, (first, n, out) in enumerate(((0, 4, out_x), (4, 4, out_y), (8, 3, out_z)))
+    ]
+    for copy in copies:
+        copy.start()
+    for copy in copies:
+        copy.wait()
+
+
+def deliver(stack):
+    return pl.pallas_call(
+        deliver_kernel,
+        out_shape=[jax.ShapeDtypeStruct((n, 16, 128), jnp.float32) for n in (4, 4, 3)],
+        in_specs=[pl.BlockSpec(memory_space=pl.ANY)],
+        out_specs=[pl.BlockSpec(memory_space=pl.ANY)] * 3,
+        scratch_shapes=[pltpu.SemaphoreType.DMA((3,))],
+    )(stack)
+
+
 def on_device(*args):
-    return compute(*exchange(*args))
+    return tuple(deliver(adjoint(*args)))
 
 
 def solution(mesh):

time: 25.6 us -> 27.4 us (1.070); the launches traced: 25.1 us -> 27.2 us
  Pallas kernels: 24.4 us -> 26.5 us
    pallas_call x2, Pallas kernels: 24.4 us -> 26.5 us  [the longest x1 22.7 us: adjoint(): pl.pallas_call(adjoint_kernel, out_shape=jax.ShapeDtypeStruct((11, 16, 12...]
where the time goes in v3:
time: 27.4 us; the launch traced here: 27.2 us
  Pallas kernels  26.5 us (97%)
  between operations  0.64 us (2%)
    pallas_call x1, Pallas kernels, adjoint(): pl.pallas_call(adjoint_kernel, out_shape=jax.ShapeDtypeStruct((11, 16, 12...  22.7 us
    pallas_call x1, Pallas kernels, deliver(): pl.pallas_call(deliver_kernel, out_shape=[jax.ShapeDtypeStruct((n, 16, 12...  3.86 us

profile of v3, /device:TPU:56, one launch (start us, length us, event | category | flops | bytes accessed | tf_op | source)
XLA Modules:
  0.0 27.2 jit_solution(7471961494622131219)
XLA Ops:
  0.6 22.7 %shard_map.130.stack = f32[11,16,128]{2,1,0:T(8,128)} custom-call(f32[4,16,128]{2,1,0:T(8,128)} %refs_0_.1, f32[4,16,128]{2,1,0:T(8,128)} %refs_1_.1, f32[4,16,128]{2,1,0:T(8,128)} %refs_2_.1, f32[4,16,128]{2,1,0:T(8,128)} %refs_3_.1, f32[3,16,128]{2,1,0:T(8,128)} %refs_4_.1, f32[4,16,128]{2,1,0:T(8,128)} %refs_5_.1, s32[4,16,128]{2,1,0:T(8,128)} %refs_6_.1, ...), custom_call_target="tpu_custom_call" | custom-call | tf_op jit(solution)/shard_map/pallas_call | solution.py:567
  23.3 3.9 %shard_map.131 = (f32[4,16,128]{2,1,0:T(8,128)}, f32[4,16,128]{2,1,0:T(8,128)}, f32[3,16,128]{2,1,0:T(8,128)}) custom-call(f32[11,16,128]{2,1,0:T(8,128)} %shard_map.130.stack), custom_call_target="tpu_custom_call" | custom-call | tf_op jit(solution)/shard_map/pallas_call | solution.py:589

commit v4 on v3

--- a/solution.py
+++ b/solution.py
@@ -18,7 +18,7 @@
     own, own_up, own_list, from_n, from_s, up_n, up_s, ext_n, ext_s = halo[:9]
     from_e, from_w, from_ne, from_nw, from_se, from_sw = halo[9:]
     cell_v, rate_v, plan_v, obs_v, xtra_n, xtra_s, pack_e, pack_w = work
-    in_sem, send_sem, recv_sem = sems
+    in_sem, send_sem, recv_sem, far_sem, near_sem = sems
     gx, gy = lax.axis_index("gx"), lax.axis_index("gy")
     nx, ny = lax.axis_size("gx"), lax.axis_size("gy")
     has_n, has_s = gx > 0, gx < nx - 1
@@ -35,9 +35,17 @@
         (both(has_s, has_w), (gx + 1, gy - 1)),
     )
     N, S, E, W, NE, NW, SE, SW = range(8)
+    far_s, far_n = gx == nx // 2 - 1, gx == nx // 2
+    herald = gx == nx // 2 - 2
+    near_s, near_n = jnp.logical_not(far_s), jnp.logical_not(far_n)
 
     barrier = pltpu.get_barrier_semaphore()
-    for here, peer in peers:
+    for at, (here, peer) in enumerate(peers):
+        if at in (E, W):
+            here = both(here, near_s)
+        elif at in (S, SE, SW):
+            here = both(here, both(near_s, jnp.logical_not(herald)))
+
         @pl.when(here)
         def _():
             pl.semaphore_signal(barrier, inc=1, device_id=peer, device_id_type=MESH)
@@ -48,6 +56,43 @@
     loads = [pltpu.make_async_copy(a, b, in_sem.at[i]) for i, (a, b) in enumerate(loads)]
     for load in loads:
         load.start()
+
+    rows = jnp.where(both(has_n, near_n), 1, 0) + jnp.where(has_s, 1, 0) + 1
+    columns = jnp.where(has_e, 1, 0) + jnp.where(has_w, 1, 0) + 1
+    pl.semaphore_wait(barrier, jnp.where(far_s, columns, rows * columns - 1))
+
+    @pl.when(herald)
+    def _():
+        pl.semaphore_signal(near_sem, inc=1, device_id=(gx + 1, gy), device_id_type=MESH)
+
+    for at in (S, SE, SW):
+        here, peer = peers[at]
+
+        @pl.when(both(here, far_s))
+        def _():
+            pl.semaphore_signal(far_sem, inc=1, device_id=peer, device_id_type=MESH)
+
+    sends = []
+
+    def send(src, dst, to, origin):
+        at = len(sends)
+        here, peer = peers[to]
+        copy = pltpu.make_async_remote_copy(
+            src_ref=src, dst_ref=dst, send_sem=send_sem.at[at], recv_sem=recv_sem.at[at],
+            device_id=peer, device_id_type=MESH,
+        )
+        sends.append((copy, to, here, peers[origin][0]))
+
+        if to in (N, NE, NW):
+            here = both(here, near_n)
+
+        @pl.when(here)
+        def _():
+            copy.start()
+
+    for ref, slot, n in fields:
+        send(ref.at[:, pl.ds(8, 8), :], from_n.at[pl.ds(slot, n)], S, N)
+    send(up.at[:, pl.ds(8, 8), :], up_n, S, N)
 
     for load in loads:
         load.wait()
@@ -104,38 +149,32 @@
             pack_e[2 + 4 * half + group] = first
             pack_w[2 + 4 * half + group] = second
 
-    rows = jnp.where(has_n, 1, 0) + jnp.where(has_s, 1, 0) + 1
-    columns = jnp.where(has_e, 1, 0) + jnp.where(has_w, 1, 0) + 1
-    pl.semaphore_wait(barrier, rows * columns - 1)
-
-    sends = []
-
-    def send(src, dst, to, origin):
-        at = len(sends)
-        here, peer = peers[to]
-        copy = pltpu.make_async_remote_copy(
-            src_ref=src, dst_ref=dst, send_sem=send_sem.at[at], recv_sem=recv_sem.at[at],
-            device_id=peer, device_id_type=MESH,
-        )
-        sends.append((copy, here, peers[origin][0]))
-
-        @pl.when(here)
-        def _():
-            copy.start()
-
+    send(xtra_n, ext_n, S, N)
     send(pack_w.at[pl.ds(6, 5)], from_nw, SE, NW)
     send(pack_e.at[pl.ds(6, 5)], from_ne, SW, NE)
+
+    @pl.when(far_s)
+    def _():
+        pl.semaphore_wait(near_sem, 1)
+
+    send(pack_w.at[pl.ds(1, 9)], from_w, E, W)
+    send(pack_e.at[pl.ds(1, 9)], from_e, W, E)
     send(pack_w.at[pl.ds(0, 6)], from_sw, NE, SW)
     send(pack_e.at[pl.ds(0, 6)], from_se, NW, SE)
     send(xtra_s, ext_s, N, S)
-    send(xtra_n, ext_n, S, N)
     send(own.at[:, pl.ds(0, 8), :], from_s, N, S)
-    send(own.at[:, pl.ds(8, 8), :], from_n, S, N)
     send(own_up.at[:, pl.ds(0, 8), :], up_s, N, S)
-    send(own_up.at[:, pl.ds(8, 8), :], up_n, S, N)
-    send(pack_w.at[pl.ds(1, 9)], from_w, E, W)
-    send(pack_e.at[pl.ds(1, 9)], from_e, W, E)
-    return sends
+
+    @pl.when(far_n)
+    def _():
+        pl.semaphore_wait(far_sem, columns)
+
+    for copy, to, here, origin in sends:
+        if to in (N, NE, NW):
+            @pl.when(both(here, far_n))
+            def _():
+                copy.start()
+    return [(copy, here, origin) for copy, to, here, origin in sends]
 
 
 def x_next(v):
@@ -563,10 +602,10 @@
         pltpu.VMEM((2, 2, 1, 1, WELLS), f32),
         tiles(2), tiles(5), tiles(11), tiles(11),
     ]
-    sems = [pltpu.SemaphoreType.DMA((n,)) for n in (11, 12, 12)]
+    sems = [pltpu.SemaphoreType.DMA((n,)) for n in (11, 17, 17)] + [pltpu.SemaphoreType.REGULAR] * 2
     return pl.pallas_call(
         adjoint_kernel,
-        out_shape=jax.ShapeDtypeStruct((11, 16, 128), f32),
+        out_shape=pltpu.VMEM((11, 16, 128), f32),
         in_specs=[pl.BlockSpec(memory_space=pl.ANY)] * 11,
         out_specs=pl.BlockSpec(memory_space=pltpu.VMEM),
         scratch_shapes=halo + work + sems,
@@ -589,10 +628,10 @@
     return pl.pallas_call(
         deliver_kernel,
         out_shape=[jax.ShapeDtypeStruct((n, 16, 128), jnp.float32) for n in (4, 4, 3)],
-        in_specs=[pl.BlockSpec(memory_space=pl.ANY)],
+        in_specs=[pl.BlockSpec(memory_space=pltpu.VMEM)],
         out_specs=[pl.BlockSpec(memory_space=pl.ANY)] * 3,
         scratch_shapes=[pltpu.SemaphoreType.DMA((3,))],
-    )(stack)
+    )(pltpu.with_memory_space_constraint(stack, pltpu.VMEM))
 
 
 def on_device(*args):

time: 27.4 us -> 20.3 us (0.74)
  the two profiles are of different devices: /device:TPU:56 before, /device:TPU:48 now
where the time goes in v4:
time: 20.3 us; the launch traced here: 20.1 us
  Pallas kernels  19.4 us (96%)
  between operations  0.64 us (3%)
    pallas_call x1, Pallas kernels, adjoint(): pl.pallas_call(adjoint_kernel, out_shape=pltpu.VMEM((11, 16, 128), f32),...  18.8 us
    pallas_call x1, Pallas kernels, deliver(): pl.pallas_call(deliver_kernel, out_shape=[jax.ShapeDtypeStruct((n, 16, 12...  0.66 us

profile of v4, /device:TPU:48, one launch (start us, length us, event | category | flops | bytes accessed | tf_op | source)
XLA Modules:
  0.0 20.1 jit_solution(2968785933077391366)
XLA Ops:
  0.6 18.8 %shard_map.130.stack = f32[11,16,128]{2,1,0:T(8,128)S(1)} custom-call(f32[4,16,128]{2,1,0:T(8,128)} %refs_0_.1, f32[4,16,128]{2,1,0:T(8,128)} %refs_1_.1, f32[4,16,128]{2,1,0:T(8,128)} %refs_2_.1, f32[4,16,128]{2,1,0:T(8,128)} %refs_3_.1, f32[3,16,128]{2,1,0:T(8,128)} %refs_4_.1, f32[4,16,128]{2,1,0:T(8,128)} %refs_5_.1, s32[4,16,128]{2,1,0:T(8,128)} %refs_6_.1, ...), custom_call_target="tpu_custom_call" | custom-call | tf_op jit(solution)/shard_map/pallas_call | solution.py:606
  19.4 0.7 %shard_map.131 = (f32[4,16,128]{2,1,0:T(8,128)}, f32[4,16,128]{2,1,0:T(8,128)}, f32[3,16,128]{2,1,0:T(8,128)}) custom-call(f32[11,16,128]{2,1,0:T(8,128)S(1)} %shard_map.130.stack), custom_call_target="tpu_custom_call" | custom-call | tf_op jit(solution)/shard_map/pallas_call | solution.py:628

commit v5 on v4

--- a/solution.py
+++ b/solution.py
@@ -8,7 +8,7 @@
 MESH = pl.DeviceIdType.MESH
 time_step = 0.05
 
-P0, S0, TX, TY, TZ, PV, UP, SLOTS = 0, 4, 8, 12, 16, 19, 23, 27
+P0, TX, TY, TZ, PV, S0, UP, SLOTS = 0, 4, 8, 12, 15, 19, 23, 27
 GROUPS = 4
 WELLS = 64
 
@@ -38,6 +38,14 @@
     far_s, far_n = gx == nx // 2 - 1, gx == nx // 2
     herald = gx == nx // 2 - 2
     near_s, near_n = jnp.logical_not(far_s), jnp.logical_not(far_n)
+    yields = both(far_s, gy < ny // 4)
+
+    fields = ((p0, P0, 4), (tx, TX, 4), (ty, TY, 4), (tz, TZ, 3), (pv, PV, 4), (s0, S0, 4))
+    loads = [(ref, own.at[pl.ds(slot, n)]) for ref, slot, n in fields]
+    loads += [(up, own_up), (cell, cell_v), (rate, rate_v), (plan, plan_v), (observed, obs_v)]
+    loads = [pltpu.make_async_copy(a, b, in_sem.at[i]) for i, (a, b) in enumerate(loads)]
+    for load in loads:
+        load.start()
 
     barrier = pltpu.get_barrier_semaphore()
     for at, (here, peer) in enumerate(peers):
@@ -50,13 +58,6 @@
         def _():
             pl.semaphore_signal(barrier, inc=1, device_id=peer, device_id_type=MESH)
 
-    fields = ((p0, P0, 4), (tx, TX, 4), (ty, TY, 4), (tz, TZ, 3), (pv, PV, 4), (s0, S0, 4))
-    loads = [(ref, own.at[pl.ds(slot, n)]) for ref, slot, n in fields]
-    loads += [(up, own_up), (cell, cell_v), (rate, rate_v), (plan, plan_v), (observed, obs_v)]
-    loads = [pltpu.make_async_copy(a, b, in_sem.at[i]) for i, (a, b) in enumerate(loads)]
-    for load in loads:
-        load.start()
-
     rows = jnp.where(both(has_n, near_n), 1, 0) + jnp.where(has_s, 1, 0) + 1
     columns = jnp.where(has_e, 1, 0) + jnp.where(has_w, 1, 0) + 1
     pl.semaphore_wait(barrier, jnp.where(far_s, columns, rows * columns - 1))
@@ -65,38 +66,63 @@
     def _():
         pl.semaphore_signal(near_sem, inc=1, device_id=(gx + 1, gy), device_id_type=MESH)
 
-    for at in (S, SE, SW):
+    for at, slot in ((S, N), (SE, NW), (SW, NE)):
         here, peer = peers[at]
 
         @pl.when(both(here, far_s))
         def _():
-            pl.semaphore_signal(far_sem, inc=1, device_id=peer, device_id_type=MESH)
+            pl.semaphore_signal(
+                far_sem.at[slot], inc=1, device_id=peer, device_id_type=MESH
+            )
 
     sends = []
 
-    def send(src, dst, to, origin):
+    def send(src, dst, to, origin, late=False):
         at = len(sends)
         here, peer = peers[to]
         copy = pltpu.make_async_remote_copy(
             src_ref=src, dst_ref=dst, send_sem=send_sem.at[at], recv_sem=recv_sem.at[at],
             device_id=peer, device_id_type=MESH,
         )
-        sends.append((copy, to, here, peers[origin][0]))
+        group = 2 if late else 0 if to in (E, W) else 1
+        sends.append((copy, to, here, peers[origin][0], group))
 
         if to in (N, NE, NW):
             here = both(here, near_n)
+        if to == S and len(sends) <= 5:
+            here = both(here, jnp.logical_not(yields))
 
         @pl.when(here)
         def _():
             copy.start()
 
-    for ref, slot, n in fields:
+    for ref, slot, n in fields[:5]:
         send(ref.at[:, pl.ds(8, 8), :], from_n.at[pl.ds(slot, n)], S, N)
-    send(up.at[:, pl.ds(8, 8), :], up_n, S, N)
-
-    for load in loads:
+
+    for load in loads[:7]:
         load.wait()
 
+    block = lax.broadcasted_iota(jnp.int32, (8, 128), 1) // 16
+
+    def pack_half(half):
+        for group in range(GROUPS):
+            first = second = None
+            for k in range(min(8, SLOTS - 8 * group)):
+                slot = 8 * group + k
+                if slot < UP:
+                    tile = own[slot, 8 * half : 8 * half + 8]
+                else:
+                    tile = own_up[slot - UP, 8 * half : 8 * half + 8].astype(jnp.float32)
+                if k:
+                    tile = pltpu.roll(tile, 16 * k, axis=1)
+                first = tile if first is None else jnp.where(block == k, tile, first)
+                second = tile if second is None else jnp.where(block == (k + 7) % 8, tile, second)
+            pack_e[2 + 4 * half + group] = first
+            pack_w[2 + 4 * half + group] = second
+
+    pack_half(1)
+    for load in loads[7:]:
+        load.wait()
     rates = rate_v[0] * 0.5
     rows = [
         cell_v[0].astype(jnp.float32),
@@ -111,6 +137,18 @@
     wells = jnp.concatenate(rows, axis=0)
     wells = jnp.concatenate([wells, wells], axis=1)
     own_list[...] = wells
+    pack_e[10] = wells
+    pack_w[10] = wells
+    send(pack_w.at[pl.ds(6, 5)], from_nw, SE, NW)
+    send(pack_e.at[pl.ds(6, 5)], from_ne, SW, NE)
+
+    for layer in range(4):
+        xtra_n[0, layer : layer + 1] = own[P0 + layer, 7:8]
+        xtra_n[0, 4 + layer : 5 + layer] = own[TX + layer, 7:8]
+    xtra_n[1] = wells
+    send(xtra_n, ext_n, S, N)
+    send(own.at[pl.ds(S0, 4), pl.ds(8, 8), :], from_n.at[pl.ds(S0, 4)], S, N, True)
+    send(own_up.at[:, pl.ds(8, 8), :], up_n, S, N, True)
 
     for layer in range(4):
         xtra_s[0, layer : layer + 1] = own[P0 + layer, 8:9]
@@ -122,36 +160,12 @@
         xtra_s[3, layer : layer + 1] = own[PV + layer, 8:9]
         if layer < 3:
             xtra_s[3, 4 + layer : 5 + layer] = own[TZ + layer, 8:9]
-        xtra_n[0, layer : layer + 1] = own[P0 + layer, 7:8]
-        xtra_n[0, 4 + layer : 5 + layer] = own[TX + layer, 7:8]
     xtra_s[3, 7:8] = jnp.zeros((1, 128), jnp.float32)
     xtra_s[4] = wells
-    xtra_n[1] = wells
-
-    block = lax.broadcasted_iota(jnp.int32, (8, 128), 1) // 16
     for pack in (pack_e, pack_w):
         pack[0] = xtra_s[0]
         pack[1] = wells
-        pack[10] = wells
-    for half in range(2):
-        for group in range(GROUPS):
-            first = second = None
-            for k in range(min(8, SLOTS - 8 * group)):
-                slot = 8 * group + k
-                if slot < UP:
-                    tile = own[slot, 8 * half : 8 * half + 8]
-                else:
-                    tile = own_up[slot - UP, 8 * half : 8 * half + 8].astype(jnp.float32)
-                if k:
-                    tile = pltpu.roll(tile, 16 * k, axis=1)
-                first = tile if first is None else jnp.where(block == k, tile, first)
-                second = tile if second is None else jnp.where(block == (k + 7) % 8, tile, second)
-            pack_e[2 + 4 * half + group] = first
-            pack_w[2 + 4 * half + group] = second
-
-    send(xtra_n, ext_n, S, N)
-    send(pack_w.at[pl.ds(6, 5)], from_nw, SE, NW)
-    send(pack_e.at[pl.ds(6, 5)], from_ne, SW, NE)
+    pack_half(0)
 
     @pl.when(far_s)
     def _():
@@ -162,19 +176,33 @@
     send(pack_w.at[pl.ds(0, 6)], from_sw, NE, SW)
     send(pack_e.at[pl.ds(0, 6)], from_se, NW, SE)
     send(xtra_s, ext_s, N, S)
-    send(own.at[:, pl.ds(0, 8), :], from_s, N, S)
-    send(own_up.at[:, pl.ds(0, 8), :], up_s, N, S)
-
-    @pl.when(far_n)
-    def _():
-        pl.semaphore_wait(far_sem, columns)
-
-    for copy, to, here, origin in sends:
+    send(own.at[pl.ds(0, S0), pl.ds(0, 8), :], from_s.at[pl.ds(0, S0)], N, S)
+    send(own.at[pl.ds(S0, 4), pl.ds(0, 8), :], from_s.at[pl.ds(S0, 4)], N, S, True)
+    send(own_up.at[:, pl.ds(0, 8), :], up_s, N, S, True)
+
+    for at in (N, NE, NW):
+        @pl.when(both(peers[at][0], far_n))
+        def _():
+            pl.semaphore_wait(far_sem.at[at], 1)
+
+    for copy, to, here, origin, group in sends:
         if to in (N, NE, NW):
             @pl.when(both(here, far_n))
             def _():
                 copy.start()
-    return [(copy, here, origin) for copy, to, here, origin in sends]
+
+    for copy, to, here, origin, group in sends:
+        if group == 0:
+            @pl.when(both(yields, here))
+            def _():
+                copy.wait_send()
+
+    @pl.when(yields)
+    def _():
+        for copy, *_ in sends[:5]:
+            copy.start()
+
+    return [(copy, both(here, jnp.logical_not(yields)) if group == 0 else here, origin, group) for copy, to, here, origin, group in sends]
 
 
 def x_next(v):
@@ -197,10 +225,9 @@
     return v[8:24, 0:128]
 
 
-def well_grids(lists_main, lists_side, missing_n, missing_s, missing_e, missing_w):
+def well_grids(lists_main, lists_side, missing_n, missing_s, missing_e, missing_w, arrive):
     lane = lax.broadcasted_iota(jnp.int32, (1, 128), 1)
     low = lane < 64
-    side = [jnp.where(low, e, w) for e, w in lists_side]
 
     def ids(cells, drop):
         cells = cells.astype(jnp.int32)
@@ -263,15 +290,20 @@
         col = jnp.where(low, jnp.where(col < 64, col, -1), jnp.where(col < 64, -1, col))
         return row, columns(col), side_values(tile)
 
-    n, c, s = [main_part(t, d) for t, d in zip(lists_main, (missing_n, 0, missing_s))]
-    sn, sc, ss = [side_part(t, d) for t, d in zip(side, (missing_n, 0, missing_s))]
-    mains = [
-        product(*n, 8, False), product(*c, 0, False), product(*c, 8, False), product(*s, 0, True)
-    ]
-    sides = [
-        product(*sn, 8, False), product(*sc, 0, False), product(*sc, 8, False),
-        product(*ss, 0, False),
-    ]
+    def both_parts(at, drop):
+        e, w = lists_side[at]()
+        return (
+            main_part(lists_main[at](), drop),
+            side_part(jnp.where(low, e, w), drop),
+        )
+
+    c, sc = both_parts(1, 0)
+    middle = [product(*part, first, False) for part in (c, sc) for first in (0, 8)]
+    arrive()
+    n, sn = both_parts(0, missing_n)
+    s, ss = both_parts(2, missing_s)
+    mains = [product(*n, 8, False), middle[0], middle[1], product(*s, 0, True)]
+    sides = [product(*sn, 8, False), middle[2], middle[3], product(*ss, 0, False)]
     grids = []
     for q in range(7):
         layers = []
@@ -296,11 +328,15 @@
     sends = start_exchange(args, halo, work, sems)
     own, own_up, own_list, from_n, from_s, up_n, up_s, ext_n, ext_s = halo[:9]
     from_e, from_w, from_ne, from_nw, from_se, from_sw = halo[9:]
-    for copy, here, origin in sends:
-        @pl.when(origin)
-        def _():
-            copy.wait_recv()
-
+
+    def receive(which):
+        for copy, here, origin, group in sends:
+            if group == which:
+                @pl.when(origin)
+                def _():
+                    copy.wait_recv()
+
+    receive(0)
     gx, gy = lax.axis_index("gx"), lax.axis_index("gy")
     nx, ny = lax.axis_size("gx"), lax.axis_size("gy")
     miss_n, miss_s = gx == 0, gx == nx - 1
@@ -318,6 +354,17 @@
     valid = row_ok & lane_ok
     keep_x = valid & jnp.logical_not((row == 23) & miss_s)
     keep_y = valid & jnp.logical_not((lane == 127) & miss_e)
+
+    (src0, src1, obs_p0, obs_s0, obs_p1, obs_s1, count), src0_extra = well_grids(
+        (lambda: ext_n[1], lambda: own_list[...], lambda: ext_s[4]),
+        (
+            lambda: (from_ne[4], from_nw[4]),
+            lambda: (from_e[0], from_w[0]),
+            lambda: (from_se[1], from_sw[1]),
+        ),
+        *[jnp.where(miss, 1, 0) for miss in (miss_n, miss_s, miss_e, miss_w)],
+        lambda: receive(1),
+    )
 
     block = lax.broadcasted_iota(jnp.int32, (8, 128), 1) // 16
     even = jnp.bitwise_and(block, 1) == 0
@@ -349,18 +396,11 @@
 
     L = range(4)
     p0 = [field(P0 + l, valid, 0.0) for l in L]
-    s0 = [field(S0 + l, valid, 0.0) for l in L]
     tx = [field(TX + l, keep_x, 0.0) for l in L]
     ty = [field(TY + l, keep_y, 0.0) for l in L]
     tz = [field(TZ + l, valid, 0.0) for l in range(3)]
     pv = [field(PV + l, valid, 1.0) for l in L]
-    up = [field(UP + l, valid, 0) for l in L]
-
-    (src0, src1, obs_p0, obs_s0, obs_p1, obs_s1, count), src0_extra = well_grids(
-        (ext_n[1], own_list[...], ext_s[4]),
-        ((from_ne[4], from_nw[4]), (from_e[0], from_w[0]), (from_se[1], from_sw[1])),
-        *[jnp.where(miss, 1, 0) for miss in (miss_n, miss_s, miss_e, miss_w)],
-    )
+
     src, obs_p, obs_s = (src0, src1), (obs_p0, obs_p1), (obs_s0, obs_s1)
 
     row8 = lax.broadcasted_iota(jnp.int32, (8, 256), 0)
@@ -426,11 +466,9 @@
     )
     q_extra = num_x / (pv_x + tx_x + txw_x + ty_x + tyw_x + tz_x + tzw_x)
 
-    bits = [[[jnp.bitwise_and(up[l], 1 << (3 * n + d)) != 0 for d in range(3)] for l in L] for n in range(2)]
-
     ipv = [time_step / pv[l] for l in L]
     saved = []
-    p, s = p0, s0
+    p = p0
     for n in range(2):
         p_next = [x_next(p[l]) for l in L]
         p_prev = [x_prev(p[l]) for l in L]
@@ -444,6 +482,12 @@
             q_next = [last_row(q_next[l], q_extra[l : l + 1]) for l in L]
         total = gather(q, q_next, [x_prev(q[l]) for l in L])
         r = [(base[l] + total[l]) * inv[l] for l in L]
+
+        if n == 0:
+            receive(2)
+            s = [field(S0 + l, valid, 0.0) for l in L]
+            up = [field(UP + l, valid, 0) for l in L]
+            bits = [[[jnp.bitwise_and(up[l], 1 << (3 * n + d)) != 0 for d in range(3)] for l in L] for n in range(2)]
 
         den = []
         mob = []
@@ -578,7 +622,7 @@
         if l < 3:
             out[8 + l] = grad_z[l]
 
-    for copy, here, origin in sends:
+    for copy, here, origin, group in sends:
         @pl.when(here)
         def _():
             copy.wait_send()
@@ -602,7 +646,9 @@
         pltpu.VMEM((2, 2, 1, 1, WELLS), f32),
         tiles(2), tiles(5), tiles(11), tiles(11),
     ]
-    sems = [pltpu.SemaphoreType.DMA((n,)) for n in (11, 17, 17)] + [pltpu.SemaphoreType.REGULAR] * 2
+    sems = [pltpu.SemaphoreType.DMA((n,)) for n in (11, 18, 18)] + [
+        pltpu.SemaphoreType.REGULAR((8,)), pltpu.SemaphoreType.REGULAR
+    ]
     return pl.pallas_call(
         adjoint_kernel,
         out_shape=pltpu.VMEM((11, 16, 128), f32),

time: 20.3 us -> 19.1 us (0.941)
  the two profiles are of different devices: /device:TPU:48 before, /device:TPU:56 now
where the time goes in v5:
time: 19.1 us; the launch traced here: 18.9 us
  Pallas kernels  18.3 us (96%)
  between operations  0.64 us (3%)
    pallas_call x1, Pallas kernels, adjoint(): pl.pallas_call(adjoint_kernel, out_shape=pltpu.VMEM((11, 16, 128), f32),...  17.6 us
    pallas_call x1, Pallas kernels, deliver(): pl.pallas_call(deliver_kernel, out_shape=[jax.ShapeDtypeStruct((n, 16, 12...  0.66 us

profile of v5, /device:TPU:56, one launch (start us, length us, event | category | flops | bytes accessed | tf_op | source)
XLA Modules:
  0.0 18.9 jit_solution(14168950167925791274)
XLA Ops:
  0.6 17.6 %shard_map.130.stack = f32[11,16,128]{2,1,0:T(8,128)S(1)} custom-call(f32[4,16,128]{2,1,0:T(8,128)} %refs_0_.1, f32[4,16,128]{2,1,0:T(8,128)} %refs_1_.1, f32[4,16,128]{2,1,0:T(8,128)} %refs_2_.1, f32[4,16,128]{2,1,0:T(8,128)} %refs_3_.1, f32[3,16,128]{2,1,0:T(8,128)} %refs_4_.1, f32[4,16,128]{2,1,0:T(8,128)} %refs_5_.1, s32[4,16,128]{2,1,0:T(8,128)} %refs_6_.1, ...), custom_call_target="tpu_custom_call" | custom-call | tf_op jit(solution)/shard_map/pallas_call | solution.py:652
  18.2 0.7 %shard_map.131 = (f32[4,16,128]{2,1,0:T(8,128)}, f32[4,16,128]{2,1,0:T(8,128)}, f32[3,16,128]{2,1,0:T(8,128)}) custom-call(f32[11,16,128]{2,1,0:T(8,128)S(1)} %shard_map.130.stack), custom_call_target="tpu_custom_call" | custom-call | tf_op jit(solution)/shard_map/pallas_call | solution.py:674

commit v6 on v5

--- a/solution.py
+++ b/solution.py
@@ -233,7 +233,7 @@
         cells = cells.astype(jnp.int32)
         row = lax.shift_right_logical(cells, 7)
         col = jnp.bitwise_and(cells, 127)
-        return row - 1024 * drop, col
+        return row * (1 - drop) - drop, col
 
     def columns(col):
         at = lax.broadcasted_iota(jnp.int32, (128, 128), 0)

time: 19.1 us -> 19.1 us (level)
  no operation moved by 1% of the time
where the time goes in v6:
time: 19.1 us; the launch traced here: 18.9 us
  Pallas kernels  18.2 us (95%)
  between operations  0.64 us (3%)
    pallas_call x1, Pallas kernels, adjoint(): pl.pallas_call(adjoint_kernel, out_shape=pltpu.VMEM((11, 16, 128), f32),...  17.6 us
    pallas_call x1, Pallas kernels, deliver(): pl.pallas_call(deliver_kernel, out_shape=[jax.ShapeDtypeStruct((n, 16, 12...  0.66 us

profile of v6, /device:TPU:56, one launch (start us, length us, event | category | flops | bytes accessed | tf_op | source)
XLA Modules:
  0.0 18.9 jit_solution(1709194438947368787)
XLA Ops:
  0.6 17.6 %shard_map.130.stack = f32[11,16,128]{2,1,0:T(8,128)S(1)} custom-call(f32[4,16,128]{2,1,0:T(8,128)} %refs_0_.1, f32[4,16,128]{2,1,0:T(8,128)} %refs_1_.1, f32[4,16,128]{2,1,0:T(8,128)} %refs_2_.1, f32[4,16,128]{2,1,0:T(8,128)} %refs_3_.1, f32[3,16,128]{2,1,0:T(8,128)} %refs_4_.1, f32[4,16,128]{2,1,0:T(8,128)} %refs_5_.1, s32[4,16,128]{2,1,0:T(8,128)} %refs_6_.1, ...), custom_call_target="tpu_custom_call" | custom-call | tf_op jit(solution)/shard_map/pallas_call | solution.py:652
  18.2 0.7 %shard_map.131 = (f32[4,16,128]{2,1,0:T(8,128)}, f32[4,16,128]{2,1,0:T(8,128)}, f32[3,16,128]{2,1,0:T(8,128)}) custom-call(f32[11,16,128]{2,1,0:T(8,128)S(1)} %shard_map.130.stack), custom_call_target="tpu_custom_call" | custom-call | tf_op jit(solution)/shard_map/pallas_call | solution.py:674

commit v7 on v6

--- a/solution.py
+++ b/solution.py
@@ -84,7 +84,7 @@
             src_ref=src, dst_ref=dst, send_sem=send_sem.at[at], recv_sem=recv_sem.at[at],
             device_id=peer, device_id_type=MESH,
         )
-        group = 2 if late else 0 if to in (E, W) else 1
+        group = 2 if late else 0 if to in (E, W) else 3 if to in (N, NE, NW) else 1
         sends.append((copy, to, here, peers[origin][0], group))
 
         if to in (N, NE, NW):
@@ -299,11 +299,13 @@
 
     c, sc = both_parts(1, 0)
     middle = [product(*part, first, False) for part in (c, sc) for first in (0, 8)]
-    arrive()
+    arrive(3)
+    s, ss = both_parts(2, missing_s)
+    lower = [product(*s, 0, True), product(*ss, 0, False)]
+    arrive(1)
     n, sn = both_parts(0, missing_n)
-    s, ss = both_parts(2, missing_s)
-    mains = [product(*n, 8, False), middle[0], middle[1], product(*s, 0, True)]
-    sides = [product(*sn, 8, False), middle[2], middle[3], product(*ss, 0, False)]
+    mains = [product(*n, 8, False), middle[0], middle[1], lower[0]]
+    sides = [product(*sn, 8, False), middle[2], middle[3], lower[1]]
     grids = []
     for q in range(7):
         layers = []
@@ -355,6 +357,30 @@
     keep_x = valid & jnp.logical_not((row == 23) & miss_s)
     keep_y = valid & jnp.logical_not((lane == 127) & miss_e)
 
+    block = lax.broadcasted_iota(jnp.int32, (8, 128), 1) // 16
+    even = jnp.bitwise_and(block, 1) == 0
+    side_tiles = {}
+
+    def unpack(j):
+        e_ref, w_ref, base = (
+            (from_ne, from_nw, 0), (from_e, from_w, 1), (from_e, from_w, 5), (from_se, from_sw, 2)
+        )[j]
+        for group in range(GROUPS):
+            e, w = e_ref[base + group], w_ref[base + group]
+            pair = jnp.where(even, e, w), jnp.where(even, w, e)
+            for k in range(min(8, SLOTS - 8 * group)):
+                tile = pair[k % 2]
+                side_tiles[8 * group + k, j] = (
+                    pltpu.roll(tile, 128 - 16 * k, axis=1) if k else tile
+                )
+
+    def arrive(which):
+        receive(which)
+        for j in (3,) if which == 3 else (0,):
+            unpack(j)
+
+    unpack(1)
+    unpack(2)
     (src0, src1, obs_p0, obs_s0, obs_p1, obs_s1, count), src0_extra = well_grids(
         (lambda: ext_n[1], lambda: own_list[...], lambda: ext_s[4]),
         (
@@ -363,27 +389,11 @@
             lambda: (from_se[1], from_sw[1]),
         ),
         *[jnp.where(miss, 1, 0) for miss in (miss_n, miss_s, miss_e, miss_w)],
-        lambda: receive(1),
+        arrive,
     )
 
-    block = lax.broadcasted_iota(jnp.int32, (8, 128), 1) // 16
-    even = jnp.bitwise_and(block, 1) == 0
-    merged = []
-    for e_ref, w_ref, base in (
-        (from_ne, from_nw, 0), (from_e, from_w, 1), (from_e, from_w, 5), (from_se, from_sw, 2)
-    ):
-        pairs = []
-        for group in range(GROUPS):
-            e, w = e_ref[base + group], w_ref[base + group]
-            pairs.append((jnp.where(even, e, w), jnp.where(even, w, e)))
-        merged.append(pairs)
-
     def field(slot, mask, fill):
-        group, k = slot // 8, slot % 8
-        sides = []
-        for j in range(4):
-            tile = merged[j][group][k % 2]
-            sides.append(pltpu.roll(tile, 128 - 16 * k, axis=1) if k else tile)
+        sides = [side_tiles[slot, j] for j in range(4)]
         if slot < UP:
             mains = [from_n[slot], own[slot], from_s[slot]]
         else:

time: 19.1 us -> 19 us (level)
  no operation moved by 1% of the time
where the time goes in v7:
time: 19 us; the launch traced here: 18.8 us
  Pallas kernels  18.2 us (96%)
  between operations  0.64 us (3%)
    pallas_call x1, Pallas kernels, adjoint(): pl.pallas_call(adjoint_kernel, out_shape=pltpu.VMEM((11, 16, 128), f32),...  17.5 us
    pallas_call x1, Pallas kernels, deliver(): pl.pallas_call(deliver_kernel, out_shape=[jax.ShapeDtypeStruct((n, 16, 12...  0.66 us

profile of v7, /device:TPU:56, one launch (start us, length us, event | category | flops | bytes accessed | tf_op | source)
XLA Modules:
  0.0 18.8 jit_solution(8992739158676444024)
XLA Ops:
  0.6 17.5 %shard_map.130.stack = f32[11,16,128]{2,1,0:T(8,128)S(1)} custom-call(f32[4,16,128]{2,1,0:T(8,128)} %refs_0_.1, f32[4,16,128]{2,1,0:T(8,128)} %refs_1_.1, f32[4,16,128]{2,1,0:T(8,128)} %refs_2_.1, f32[4,16,128]{2,1,0:T(8,128)} %refs_3_.1, f32[3,16,128]{2,1,0:T(8,128)} %refs_4_.1, f32[4,16,128]{2,1,0:T(8,128)} %refs_5_.1, s32[4,16,128]{2,1,0:T(8,128)} %refs_6_.1, ...), custom_call_target="tpu_custom_call" | custom-call | tf_op jit(solution)/shard_map/pallas_call | solution.py:662
  18.2 0.7 %shard_map.131 = (f32[4,16,128]{2,1,0:T(8,128)}, f32[4,16,128]{2,1,0:T(8,128)}, f32[3,16,128]{2,1,0:T(8,128)}) custom-call(f32[11,16,128]{2,1,0:T(8,128)S(1)} %shard_map.130.stack), custom_call_target="tpu_custom_call" | custom-call | tf_op jit(solution)/shard_map/pallas_call | solution.py:684
